TPU v7x, 32 devices: a whole 2x2x4 slice. The times are simulated.
32 devices in a mesh: groups: 2 (over y), segment: 2 (over core), seq: 8 (over z, x).
Axes of the slice: x: 2, y: 2, z: 4, core: 2. Of those that a mesh axis runs over, the one named last changes fastest.
Arguments:
- held: bfloat16 [2, 32, 8, 16, 640], P('segment', ('groups', 'seq')), parts along dimension 1, may hold values from -6 to 6
- arrivals: bfloat16 [3, 32, 8, 16, 640], P(None, ('groups', 'seq')), parts along dimension 1, may hold values from -6 to 6
- spatial_weight: bfloat16 [2, 9, 640, 640], P('segment'), may hold values from -0.078125 to 0.078125
- spatial_scale: float32 [2, 5, 640], P('segment'), may hold values from 0.5 to 2
- temporal_weight: bfloat16 [2, 3, 640, 640], P('segment'), may hold values from -0.125 to 0.125
- temporal_scale: float32 [2, 5, 640], P('segment'), may hold values from 0.5 to 2
Outputs:
- emitted: bfloat16 [2, 4, 32, 8, 16, 640], P('segment', None, ('groups', 'seq')), parts along dimension 2
There are 2 independent parts, one for each index of `groups`. A program takes and returns all parts, laid end to end along the dimension named above; an argument that names none is the same for every part. Nothing has to cross between parts.
All inputs are finite; a program needn't handle non-finite values.
Results may differ from a plain program's by a relative error of at most 0.014.
Values may be sent and summed in bfloat16 or wider, within the bound.
No kernel may reach another device: no remote copies, remote signals or barrier semaphores. Data moves between devices by JAX's collectives and lax.ppermute only.
A program may use at most 128 MiB of HBM per device.

v0:
```python
import jax
import jax.numpy as jnp
from jax import lax
from jax.sharding import PartitionSpec as P


def with_halo(cells, sides, width):
    for axis, dim in sides:
        count = lax.axis_size(axis)
        ends = count - 1
        head = lax.slice_in_dim(cells, 0, width, axis=dim)
        tail = lax.slice_in_dim(cells, cells.shape[dim] - width, cells.shape[dim], axis=dim)
        cells = jnp.concatenate(
            [
                lax.ppermute(tail, axis, [(i, (i + 1) % count) for i in range(ends)]),
                cells,
                lax.ppermute(head, axis, [((i + 1) % count, i) for i in range(ends)]),
            ],
            axis=dim,
        )
    return cells


def passed_along(value, axis, steps):
    count = lax.axis_size(axis)
    initial, last = (max(0, -steps), min(count, count - steps))
    return lax.ppermute(value, axis, [(source, source + steps) for source in range(initial, last)])


def dequantize(weights, scales):
    block = weights.shape[1] // scales.shape[0]
    expanded = jnp.repeat(scales, block, axis=0)
    return (weights.astype(jnp.float32) * expanded[None]).astype(jnp.bfloat16)


def spatial_term(activation, kernels):
    frames, height, width, channels = activation.shape
    padded = jnp.pad(activation, ((0, 0), (1, 1), (1, 1), (0, 0)))
    total = jnp.zeros((frames * height * width, channels), jnp.float32)
    for row_tap in range(3):
        for col_tap in range(3):
            window = padded[:, row_tap : row_tap + height, col_tap : col_tap + width].reshape(
                -1, channels
            )
            total = total + jnp.dot(
                window, kernels[row_tap * 3 + col_tap], preferred_element_type=jnp.float32
            )
    return total.reshape(activation.shape)


def section_local(activation, spatial_kernels, temporal_kernels):
    lifted = jax.nn.silu(activation.astype(jnp.float32)).astype(jnp.bfloat16)
    middle = (activation.astype(jnp.float32) + spatial_term(lifted, spatial_kernels)).astype(
        jnp.bfloat16
    )
    lifted_mid = jax.nn.silu(middle.astype(jnp.float32)).astype(jnp.bfloat16)
    frames_dev, height, width, channels = lifted_mid.shape
    extended = with_halo(lifted_mid, (("seq", 0),), 1)
    total = jnp.zeros((frames_dev * height * width, channels), jnp.float32)
    for frame_tap in range(3):
        window = extended[frame_tap : frame_tap + frames_dev].reshape(-1, channels)
        total = total + jnp.dot(
            window, temporal_kernels[frame_tap], preferred_element_type=jnp.float32
        )
    temporal = total.reshape(lifted_mid.shape).astype(jnp.bfloat16)
    return (middle.astype(jnp.float32) + temporal.astype(jnp.float32)).astype(jnp.bfloat16)


def local(held, arrivals, spatial_weight, spatial_scale, temporal_weight, temporal_scale):
    spatial_kernels = dequantize(spatial_weight[0], spatial_scale[0])
    temporal_kernels = dequantize(temporal_weight[0], temporal_scale[0])
    first_segment = lax.axis_index("segment") == 0
    ticks = arrivals.shape[0] + 1
    current = held[0]
    collected = []
    for tick_index in range(ticks):
        current = section_local(current, spatial_kernels, temporal_kernels)
        collected.append(current)
        if tick_index + 1 < ticks:
            moved = passed_along(current, "segment", 1)
            current = jnp.where(first_segment, arrivals[tick_index], moved)
    return jnp.stack(collected)[None]


def solution(mesh):
    in_specs = (
        P("segment", ("groups", "seq"), None, None, None),
        P(None, ("groups", "seq"), None, None, None),
        P("segment", None, None, None),
        P("segment", None, None),
        P("segment", None, None, None),
        P("segment", None, None),
    )
    out_specs = P("segment", None, ("groups", "seq"), None, None, None)
    return jax.shard_map(local, mesh=mesh, in_specs=in_specs, out_specs=out_specs, check_vma=False)
```

profile of v0, /device:TPU:29, one launch (start us, length us, event | category | flops | bytes accessed | tf_op | source)
XLA Modules:
  0.0 105.6 jit_solution(9680626531610827760)
XLA Ops:
  0.0 1.2 %fusion.59 = bf16[2,8,16,640]{3,2,1,0:T(8,128)(2,1)S(1)} fusion(bf16[1,2,8,16,640]{4,3,2,1,0:T(8,128)(2,1)} %param.6), kind=kLoop, calls=%fused_computation.172 | loop fusion | flops 983040 | bytes 655360 | tf_op jit(solution)/shard_map/convert_element_type | solution.py:52
  1.2 1.2 %fusion.54 = bf16[1,2,8,16,640]{4,3,2,1,0:T(8,128)(2,1)S(1)} fusion(bf16[1,2,8,16,640]{4,3,2,1,0:T(8,128)(2,1)} %param.6), kind=kLoop, calls=%fused_computation.167 | loop fusion | flops 983040 | bytes 655360 | tf_op jit(solution)/shard_map/convert_element_type | solution.py:52
  2.3 0.7 copy.12
  3.1 1.5 %pad_slice_fusion.24 = (bf16[2,8,16,640]{3,2,1,0:T(8,128)(2,1)}, bf16[2,8,16,640]{3,2,1,0:T(8,128)(2,1)S(1)}, bf16[2,8,16,640]{3,2,1,0:T(8,128)(2,1)}, bf16[2,8,...) fusion(bf16[2,8,16,640]{3,2,1,0:T(8,128)(2,1)S(1)} %fusion.59), kind=kLoop, calls=%fused_computation.74 | loop fusion | bytes 2949120 | tf_op jit(solution)/shard_map/slice | solution.py:42
  4.5 1.3 %broadcast_in_dim.9 = f32[5,128,640]{2,1,0:T(8,128)} broadcast(f32[5,640]{1,0:T(8,128)S(1)} %bitcast.310), dimensions={0,2} | broadcast | bytes 1651200 | tf_op jit(solution)/shard_map/broadcast_in_dim | solution.py:32
  5.8 5.0 %fusion = bf16[9,640,640]{2,1,0:T(8,128)(2,1)S(1)} fusion(bf16[1,9,640,640]{3,2,1,0:T(8,128)(2,1)} %param.8, f32[640,640]{1,0:T(8,128)} %bitcast.252), kind=kLoop, calls=%fused_computation.1 | loop fusion | flops 11059200 | bytes 16384000 | tf_op jit(solution)/shard_map/convert_element_type | solution.py:33
  10.8 1.8 %fusion.64 = f32[256,640]{1,0:T(8,128)S(1)} fusion(bf16[256,640]{1,0:T(8,128)(2,1)} %bitcast.291, bf16[9,640,640]{2,1,0:T(8,128)(2,1)S(1)} %fusion), kind=kOutput, calls=%fused_computation.178 | convolution fusion | flops 209715200 | bytes 1802240 | tf_op jit(solution)/shard_map/dot_general | solution.py:45
  13.1 1.8 %convolution_add_fusion.34 = f32[256,640]{1,0:T(8,128)S(1)} fusion(f32[256,640]{1,0:T(8,128)S(1)} %convolution_add_fusion.35, bf16[256,640]{1,0:T(8,128)(2,1)} %bitcast.289, bf16[9,640,640]{2,1,0:T(8,128)(2,1)S(1)} %fusion), kind=kOutput, calls=%fused_computation.39 | convolution fusion | flops 209879040 | bytes 2457600 | tf_op jit(solution)/shard_map/dot_general | solution.py:45
  14.9 1.4 %convolution_add_fusion.33 = f32[256,640]{1,0:T(8,128)S(1)} fusion(f32[256,640]{1,0:T(8,128)S(1)} %convolution_add_fusion.34, bf16[256,640]{1,0:T(8,128)(2,1)} %bitcast.285, bf16[9,640,640]{2,1,0:T(8,128)(2,1)S(1)} %fusion), kind=kOutput, calls=%fused_computation.38 | convolution fusion | flops 209879040 | bytes 2457600 | tf_op jit(solution)/shard_map/dot_general | solution.py:45
  16.8 0.5 convolution_add_fusion.31
  17.3 0.5 convolution_add_fusion.30
  17.8 0.5 convolution_add_fusion.29
  18.3 0.5 fusion.50
  19.0 3.1 %collective-permute-start = (bf16[1,8,16,640]{3,2,1,0:T(8,128)(2,1)S(1)}, bf16[1,8,16,640]{3,2,1,0:T(8,128)(2,1)S(1)}, u32[]{:S(2)}, u32[]{:S(2)}) collective-permute-start(bf16[1,8,16,640]{3,2,1,0:T(8,128)(2,1)S(1)} %get-tuple-element.49), channel_id=1, source_target_pairs={{0,1},{1,2},{2,3},{3,4},{4,5},{5,6},{6,7},{8,9},{9,10},{10,11},{11... | collective-permute-start | bytes 491528 | tf_op jit(solution)/shard_map/ppermute | solution.py:15
  22.2 3.1 %collective-permute-start.1 = (bf16[1,8,16,640]{3,2,1,0:T(8,128)(2,1)S(1)}, bf16[1,8,16,640]{3,2,1,0:T(8,128)(2,1)S(1)}, u32[]{:S(2)}, u32[]{:S(2)}) collective-permute-start(bf16[1,8,16,640]{3,2,1,0:T(8,128)(2,1)S(1)} %get-tuple-element.50), channel_id=1, source_target_pairs={{1,0},{2,1},{3,2},{4,3},{5,4},{6,5},{7,6},{9,8},{10,9},{11,10},{12... | collective-permute-start | bytes 491528 | tf_op jit(solution)/shard_map/ppermute | solution.py:17
  25.4 0.5 fusion.1
  25.9 0.5 fusion.68
  26.4 0.5 collective-permute-done
  26.9 4.5 %collective-permute-done.1 = bf16[1,8,16,640]{3,2,1,0:T(8,128)(2,1)S(1)} collective-permute-done((bf16[1,8,16,640]{3,2,1,0:T(8,128)(2,1)S(1)}, bf16[1,8,16,640]{3,2,1,0:T(8,128)(2,1)S(1)}, u32[]{:S(2)}, u32[]{:S(2)}) %collective-permute-start.1) | collective-permute-done | bytes 163872 | tf_op jit(solution)/shard_map/ppermute | solution.py:17
  32.0 0.5 fusion.10
  32.5 0.9 fusion.19
  33.4 1.3 %collective-permute-start.2 = (bf16[2,8,16,640]{3,2,1,0:T(8,128)(2,1)}, bf16[2,8,16,640]{3,2,1,0:T(8,128)(2,1)}, u32[]{:S(2)}, u32[]{:S(2)}) collective-permute-start(bf16[2,8,16,640]{3,2,1,0:T(8,128)(2,1)} %fusion.19), channel_id=1, source_target_pairs={{0,8},{1,9},{2,10},{3,11},{4,12},{5,13},{6,14},{7,15},{16,24},{17,... | collective-permute-start | bytes 983048 | tf_op jit(solution)/shard_map/ppermute | solution.py:27
  34.7 2.5 %collective-permute-done.2 = bf16[2,8,16,640]{3,2,1,0:T(8,128)(2,1)} collective-permute-done((bf16[2,8,16,640]{3,2,1,0:T(8,128)(2,1)}, bf16[2,8,16,640]{3,2,1,0:T(8,128)(2,1)}, u32[]{:S(2)}, u32[]{:S(2)}) %collective-permute-start.2) | collective-permute-done | bytes 327712 | tf_op jit(solution)/shard_map/ppermute | solution.py:27
  37.3 1.3 %fusion.23 = bf16[2,8,16,640]{3,2,1,0:T(8,128)(2,1)S(1)} fusion(bf16[2,8,16,640]{3,2,1,0:T(8,128)(2,1)} %collective-permute-done.2, bf16[3,2,8,16,640]{4,3,2,1,0:T(8,128)(2,1)} %param.7, pred[]{:T(512)S(6)} %eq.3), kind=kLoop, calls=%fused_computation.129 | loop fusion | flops 1146880 | bytes 983041 | tf_op jit(solution)/shard_map/convert_element_type | solution.py:52
  38.8 1.6 %fusion.63 = f32[256,640]{1,0:T(8,128)S(1)} fusion(bf16[256,640]{1,0:T(8,128)(2,1)S(1)} %bitcast.301, bf16[9,640,640]{2,1,0:T(8,128)(2,1)} %copy-done), kind=kOutput, calls=%fused_computation.177 | convolution fusion | flops 209715200 | bytes 1802240 | tf_op jit(solution)/shard_map/dot_general | solution.py:45
  40.4 1.6 %convolution_add_fusion.26 = f32[256,640]{1,0:T(8,128)S(1)} fusion(f32[256,640]{1,0:T(8,128)S(1)} %fusion.63, bf16[256,640]{1,0:T(8,128)(2,1)S(1)} %bitcast.298, bf16[9,640,640]{2,1,0:T(8,128)(2,1)} %copy-done), kind=kOutput, calls=%fused_computation.31 | convolution fusion | flops 209879040 | bytes 2457600 | tf_op jit(solution)/shard_map/dot_general | solution.py:45
  42.1 0.5 convolution_add_fusion.25
  45.4 1.2 %fusion.28 = (bf16[2,8,16,640]{3,2,1,0:T(8,128)(2,1)S(1)}, bf16[2,8,16,640]{3,2,1,0:T(8,128)(2,1)S(1)}) fusion(f32[2,8,16,640]{3,2,1,0:T(8,128)S(1)} %bitcast.262, bf16[2,8,16,640]{3,2,1,0:T(8,128)(2,1)} %collective-permute-done.2, bf16[3,2,8,16,640]{4,3,2,1,0:T(8,128)(2,1)S(1)} %copy-done.8, pred[]{:T(512)S(6)} %eq.3), kind=kLoop, calls=%fused_computation.134 | loop fusion | flops 1638400 | bytes 1966081 | tf_op jit(solution)/shard_map/convert_element_type | solution.py:56
  46.6 1.9 %collective-permute-start.3 = (bf16[1,8,16,640]{3,2,1,0:T(8,128)(2,1)S(1)}, bf16[1,8,16,640]{3,2,1,0:T(8,128)(2,1)S(1)}, u32[]{:S(2)}, u32[]{:S(2)}) collective-permute-start(bf16[1,8,16,640]{3,2,1,0:T(8,128)(2,1)S(1)} %get-tuple-element.37), channel_id=1, source_target_pairs={{0,1},{1,2},{2,3},{3,4},{4,5},{5,6},{6,7},{8,9},{9,10},{10,11},{11... | collective-permute-start | bytes 491528 | tf_op jit(solution)/shard_map/ppermute | solution.py:15
  48.6 4.4 %collective-permute-start.4 = (bf16[1,8,16,640]{3,2,1,0:T(8,128)(2,1)S(1)}, bf16[1,8,16,640]{3,2,1,0:T(8,128)(2,1)S(1)}, u32[]{:S(2)}, u32[]{:S(2)}) collective-permute-start(bf16[1,8,16,640]{3,2,1,0:T(8,128)(2,1)S(1)} %get-tuple-element.38), channel_id=1, source_target_pairs={{1,0},{2,1},{3,2},{4,3},{5,4},{6,5},{7,6},{9,8},{10,9},{11,10},{12... | collective-permute-start | bytes 491528 | tf_op jit(solution)/shard_map/ppermute | solution.py:17
  53.5 2.0 %collective-permute-done.3 = bf16[1,8,16,640]{3,2,1,0:T(8,128)(2,1)S(1)} collective-permute-done((bf16[1,8,16,640]{3,2,1,0:T(8,128)(2,1)S(1)}, bf16[1,8,16,640]{3,2,1,0:T(8,128)(2,1)S(1)}, u32[]{:S(2)}, u32[]{:S(2)}) %collective-permute-start.3) | collective-permute-done | bytes 163872 | tf_op jit(solution)/shard_map/ppermute | solution.py:15
  55.5 3.5 %collective-permute-done.4 = bf16[1,8,16,640]{3,2,1,0:T(8,128)(2,1)S(1)} collective-permute-done((bf16[1,8,16,640]{3,2,1,0:T(8,128)(2,1)S(1)}, bf16[1,8,16,640]{3,2,1,0:T(8,128)(2,1)S(1)}, u32[]{:S(2)}, u32[]{:S(2)}) %collective-permute-start.4) | collective-permute-done | bytes 163872 | tf_op jit(solution)/shard_map/ppermute | solution.py:17
  59.6 0.5 fusion.8
  60.2 1.3 %collective-permute-start.5 = (bf16[2,8,16,640]{3,2,1,0:T(8,128)(2,1)S(1)}, bf16[2,8,16,640]{3,2,1,0:T(8,128)(2,1)S(1)}, u32[]{:S(2)}, u32[]{:S(2)}) collective-permute-start(bf16[2,8,16,640]{3,2,1,0:T(8,128)(2,1)S(1)} %fusion.29), channel_id=1, source_target_pairs={{0,8},{1,9},{2,10},{3,11},{4,12},{5,13},{6,14},{7,15},{16,24},{17,... | collective-permute-start | bytes 983048 | tf_op jit(solution)/shard_map/ppermute | solution.py:27
  61.5 2.2 %collective-permute-done.5 = bf16[2,8,16,640]{3,2,1,0:T(8,128)(2,1)S(1)} collective-permute-done((bf16[2,8,16,640]{3,2,1,0:T(8,128)(2,1)S(1)}, bf16[2,8,16,640]{3,2,1,0:T(8,128)(2,1)S(1)}, u32[]{:S(2)}, u32[]{:S(2)}) %collective-permute-start.5) | collective-permute-done | bytes 327712 | tf_op jit(solution)/shard_map/ppermute | solution.py:27
  68.7 1.9 %collective-permute-start.6 = (bf16[1,8,16,640]{3,2,1,0:T(8,128)(2,1)S(1)}, bf16[1,8,16,640]{3,2,1,0:T(8,128)(2,1)S(1)}, u32[]{:S(2)}, u32[]{:S(2)}) collective-permute-start(bf16[1,8,16,640]{3,2,1,0:T(8,128)(2,1)S(1)} %get-tuple-element.25), channel_id=1, source_target_pairs={{0,1},{1,2},{2,3},{3,4},{4,5},{5,6},{6,7},{8,9},{9,10},{10,11},{11... | collective-permute-start | bytes 491528 | tf_op jit(solution)/shard_map/ppermute | solution.py:15
  70.6 4.3 %collective-permute-start.7 = (bf16[1,8,16,640]{3,2,1,0:T(8,128)(2,1)S(1)}, bf16[1,8,16,640]{3,2,1,0:T(8,128)(2,1)S(1)}, u32[]{:S(2)}, u32[]{:S(2)}) collective-permute-start(bf16[1,8,16,640]{3,2,1,0:T(8,128)(2,1)S(1)} %get-tuple-element.26), channel_id=1, source_target_pairs={{1,0},{2,1},{3,2},{4,3},{5,4},{6,5},{7,6},{9,8},{10,9},{11,10},{12... | collective-permute-start | bytes 491528 | tf_op jit(solution)/shard_map/ppermute | solution.py:17
  75.4 1.8 %collective-permute-done.6 = bf16[1,8,16,640]{3,2,1,0:T(8,128)(2,1)S(1)} collective-permute-done((bf16[1,8,16,640]{3,2,1,0:T(8,128)(2,1)S(1)}, bf16[1,8,16,640]{3,2,1,0:T(8,128)(2,1)S(1)}, u32[]{:S(2)}, u32[]{:S(2)}) %collective-permute-start.6) | collective-permute-done | bytes 163872 | tf_op jit(solution)/shard_map/ppermute | solution.py:15
  77.2 4.0 %collective-permute-done.7 = bf16[1,8,16,640]{3,2,1,0:T(8,128)(2,1)S(1)} collective-permute-done((bf16[1,8,16,640]{3,2,1,0:T(8,128)(2,1)S(1)}, bf16[1,8,16,640]{3,2,1,0:T(8,128)(2,1)S(1)}, u32[]{:S(2)}, u32[]{:S(2)}) %collective-permute-start.7) | collective-permute-done | bytes 163872 | tf_op jit(solution)/shard_map/ppermute | solution.py:17
  81.7 0.5 fusion.7
  82.3 1.3 %collective-permute-start.8 = (bf16[2,8,16,640]{3,2,1,0:T(8,128)(2,1)S(1)}, bf16[2,8,16,640]{3,2,1,0:T(8,128)(2,1)S(1)}, u32[]{:S(2)}, u32[]{:S(2)}) collective-permute-start(bf16[2,8,16,640]{3,2,1,0:T(8,128)(2,1)S(1)} %fusion.39), channel_id=1, source_target_pairs={{0,8},{1,9},{2,10},{3,11},{4,12},{5,13},{6,14},{7,15},{16,24},{17,... | collective-permute-start | bytes 983048 | tf_op jit(solution)/shard_map/ppermute | solution.py:27
  83.7 2.1 %collective-permute-done.8 = bf16[2,8,16,640]{3,2,1,0:T(8,128)(2,1)S(1)} collective-permute-done((bf16[2,8,16,640]{3,2,1,0:T(8,128)(2,1)S(1)}, bf16[2,8,16,640]{3,2,1,0:T(8,128)(2,1)S(1)}, u32[]{:S(2)}, u32[]{:S(2)}) %collective-permute-start.8) | collective-permute-done | bytes 327712 | tf_op jit(solution)/shard_map/ppermute | solution.py:27
  90.8 1.9 %collective-permute-start.9 = (bf16[1,8,16,640]{3,2,1,0:T(8,128)(2,1)S(1)}, bf16[1,8,16,640]{3,2,1,0:T(8,128)(2,1)S(1)}, u32[]{:S(2)}, u32[]{:S(2)}) collective-permute-start(bf16[1,8,16,640]{3,2,1,0:T(8,128)(2,1)S(1)} %get-tuple-element.13), channel_id=1, source_target_pairs={{0,1},{1,2},{2,3},{3,4},{4,5},{5,6},{6,7},{8,9},{9,10},{10,11},{11... | collective-permute-start | bytes 491528 | tf_op jit(solution)/shard_map/ppermute | solution.py:15
  92.7 4.3 %collective-permute-start.10 = (bf16[1,8,16,640]{3,2,1,0:T(8,128)(2,1)S(1)}, bf16[1,8,16,640]{3,2,1,0:T(8,128)(2,1)S(1)}, u32[]{:S(2)}, u32[]{:S(2)}) collective-permute-start(bf16[1,8,16,640]{3,2,1,0:T(8,128)(2,1)S(1)} %get-tuple-element.14), channel_id=1, source_target_pairs={{1,0},{2,1},{3,2},{4,3},{5,4},{6,5},{7,6},{9,8},{10,9},{11,10},{12... | collective-permute-start | bytes 491528 | tf_op jit(solution)/shard_map/ppermute | solution.py:17
  97.4 1.8 %collective-permute-done.9 = bf16[1,8,16,640]{3,2,1,0:T(8,128)(2,1)S(1)} collective-permute-done((bf16[1,8,16,640]{3,2,1,0:T(8,128)(2,1)S(1)}, bf16[1,8,16,640]{3,2,1,0:T(8,128)(2,1)S(1)}, u32[]{:S(2)}, u32[]{:S(2)}) %collective-permute-start.9) | collective-permute-done | bytes 163872 | tf_op jit(solution)/shard_map/ppermute | solution.py:15
  99.2 4.0 %collective-permute-done.10 = bf16[1,8,16,640]{3,2,1,0:T(8,128)(2,1)S(1)} collective-permute-done((bf16[1,8,16,640]{3,2,1,0:T(8,128)(2,1)S(1)}, bf16[1,8,16,640]{3,2,1,0:T(8,128)(2,1)S(1)}, u32[]{:S(2)}, u32[]{:S(2)}) %collective-permute-start.10) | collective-permute-done | bytes 163872 | tf_op jit(solution)/shard_map/ppermute | solution.py:17
  103.8 0.5 fusion.6
  104.3 1.3 %maximum_bitcast_fusion = bf16[1,4,2,8,16,640]{5,4,3,2,1,0:T(8,128)(2,1)} fusion(bf16[1,2,8,16,640]{4,3,2,1,0:T(8,128)(2,1)S(1)} %fusion.74, bf16[1,2,8,16,640]{4,3,2,1,0:T(8,128)(2,1)S(1)} %bitcast.271, bf16[1,2,8,16,640]{4,3,2,1,0:T(8,128)(2,1)S(1)} %bitcast.270, bf16[1,2,8,16,640]{4,3,2,1,0:T(8,128)(2,1)S(1)} %add_convert_fusion), kind=kLoop, calls=%fused_computation.4 | loop fusion | flops 1966080 | bytes 2621440 | tf_op jit(solution)/shard_map/broadcast_in_dim | solution.py:82
  (90 shorter events, 18.1 us)
Async XLA Ops:
  10.8 7.5 %copy-start = (bf16[9,640,640]{2,1,0:T(8,128)(2,1)}, bf16[9,640,640]{2,1,0:T(8,128)(2,1)S(1)}, u32[]{:S(2)}) copy-start(bf16[9,640,640]{2,1,0:T(8,128)(2,1)S(1)} %fusion) | copy-start | bytes 22118404
  10.8 6.0 %copy-start.13 = (bf16[2,8,16,640]{3,2,1,0:T(8,128)(2,1)S(1)}, bf16[2,8,16,640]{3,2,1,0:T(8,128)(2,1)}, u32[]{:S(2)}) copy-start(bf16[2,8,16,640]{3,2,1,0:T(8,128)(2,1)} %get-tuple-element.55) | copy-start | bytes 983044
  10.8 6.5 %copy-start.12 = (bf16[2,8,16,640]{3,2,1,0:T(8,128)(2,1)S(1)}, bf16[2,8,16,640]{3,2,1,0:T(8,128)(2,1)}, u32[]{:S(2)}) copy-start(bf16[2,8,16,640]{3,2,1,0:T(8,128)(2,1)} %get-tuple-element.56) | copy-start | bytes 983044
  12.6 5.2 %copy-start.11 = (bf16[2,8,16,640]{3,2,1,0:T(8,128)(2,1)S(1)}, bf16[2,8,16,640]{3,2,1,0:T(8,128)(2,1)}, u32[]{:S(2)}) copy-start(bf16[2,8,16,640]{3,2,1,0:T(8,128)(2,1)} %get-tuple-element.57) | copy-start | bytes 983044
  13.1 5.2 %copy-start.3 = (bf16[1,2,8,16,640]{4,3,2,1,0:T(8,128)(2,1)S(1)}, bf16[1,2,8,16,640]{4,3,2,1,0:T(8,128)(2,1)}, u32[]{:S(2)}) copy-start(bf16[1,2,8,16,640]{4,3,2,1,0:T(8,128)(2,1)} %param.6) | copy-start | bytes 983044
  13.1 5.2 %copy-start.10 = (bf16[2,8,16,640]{3,2,1,0:T(8,128)(2,1)S(1)}, bf16[2,8,16,640]{3,2,1,0:T(8,128)(2,1)}, u32[]{:S(2)}) copy-start(bf16[2,8,16,640]{3,2,1,0:T(8,128)(2,1)} %get-tuple-element.51) | copy-start | bytes 983044
  16.3 8.9 %copy-start.14 = (f32[1,5,640]{2,0,1:T(1,128)S(1)}, f32[1,5,640]{2,0,1:T(1,128)}, u32[]{:S(2)}) copy-start(f32[1,5,640]{2,0,1:T(1,128)} %param.11) | copy-start | bytes 38404
  16.8 8.5 %copy-start.9 = (bf16[1,3,640,640]{3,2,1,0:T(8,128)(2,1)S(1)}, bf16[1,3,640,640]{3,2,1,0:T(8,128)(2,1)}, u32[]{:S(2)}) copy-start(bf16[1,3,640,640]{3,2,1,0:T(8,128)(2,1)} %param.10) | copy-start | bytes 7372804
  18.8 13.7 %copy-start.4 = (f32[256,640]{1,0:T(8,128)}, f32[256,640]{1,0:T(8,128)S(1)}, u32[]{:S(2)}) copy-start(f32[256,640]{1,0:T(8,128)S(1)} %get-tuple-element.60) | copy-start | bytes 1966084
  19.0 7.9 %collective-permute-start = (bf16[1,8,16,640]{3,2,1,0:T(8,128)(2,1)S(1)}, bf16[1,8,16,640]{3,2,1,0:T(8,128)(2,1)S(1)}, u32[]{:S(2)}, u32[]{:S(2)}) collective-permute-start(bf16[1,8,16,640]{3,2,1,0:T(8,128)(2,1)S(1)} %get-tuple-element.49), channel_id=1, source_target_pairs={{0,1},{1,2},{2,3},{3,4},{4,5},{5,6},{6,7},{8,9},{9,10},{10,11},{11... | collective-permute-start | bytes 491528 | tf_op jit(solution)/shard_map/ppermute | solution.py:15
  22.2 9.3 %collective-permute-start.1 = (bf16[1,8,16,640]{3,2,1,0:T(8,128)(2,1)S(1)}, bf16[1,8,16,640]{3,2,1,0:T(8,128)(2,1)S(1)}, u32[]{:S(2)}, u32[]{:S(2)}) collective-permute-start(bf16[1,8,16,640]{3,2,1,0:T(8,128)(2,1)S(1)} %get-tuple-element.50), channel_id=1, source_target_pairs={{1,0},{2,1},{3,2},{4,3},{5,4},{6,5},{7,6},{9,8},{10,9},{11,10},{12... | collective-permute-start | bytes 491528 | tf_op jit(solution)/shard_map/ppermute | solution.py:17
  25.9 6.1 %copy-start.1 = (bf16[3,640,640]{2,1,0:T(8,128)(2,1)}, bf16[3,640,640]{2,1,0:T(8,128)(2,1)S(1)}, u32[]{:S(2)}) copy-start(bf16[3,640,640]{2,1,0:T(8,128)(2,1)S(1)} %fusion.1) | copy-start | bytes 7372804
  31.5 10.5 %slice-start = ((s8[7372800]{0:T(1024)(128)(4,1)}), s8[3178496]{0:T(1024)(128)(4,1)S(1)}, s32[]{:S(2)}) async-start(s8[7372800]{0:T(1024)(128)(4,1)} %bitcast.246), calls=%async_computation | async-start | bytes 6356992
  32.5 0.9 copy-start.6
  33.4 3.9 %collective-permute-start.2 = (bf16[2,8,16,640]{3,2,1,0:T(8,128)(2,1)}, bf16[2,8,16,640]{3,2,1,0:T(8,128)(2,1)}, u32[]{:S(2)}, u32[]{:S(2)}) collective-permute-start(bf16[2,8,16,640]{3,2,1,0:T(8,128)(2,1)} %fusion.19), channel_id=1, source_target_pairs={{0,8},{1,9},{2,10},{3,11},{4,12},{5,13},{6,14},{7,15},{16,24},{17,... | collective-permute-start | bytes 983048 | tf_op jit(solution)/shard_map/ppermute | solution.py:27
  34.7 7.3 %slice-start.1 = ((s8[7372800]{0:T(1024)(128)(4,1)}), s8[4194304]{0:T(1024)(128)(4,1)S(1)}, s32[]{:S(2)}) async-start(s8[7372800]{0:T(1024)(128)(4,1)} %bitcast.246), calls=%async_computation.1 | async-start | bytes 8388608
  42.5 2.8 %copy-start.8 = (bf16[3,2,8,16,640]{4,3,2,1,0:T(8,128)(2,1)S(1)}, bf16[3,2,8,16,640]{4,3,2,1,0:T(8,128)(2,1)}, u32[]{:S(2)}) copy-start(bf16[3,2,8,16,640]{4,3,2,1,0:T(8,128)(2,1)} %param.7) | copy-start | bytes 2949124
  43.0 10.0 %copy-start.2 = (bf16[3,640,640]{2,1,0:T(8,128)(2,1)S(1)}, bf16[3,640,640]{2,1,0:T(8,128)(2,1)}, u32[]{:S(2)}) copy-start(bf16[3,640,640]{2,1,0:T(8,128)(2,1)} %copy-done.1) | copy-start | bytes 7372804
  46.6 8.9 %collective-permute-start.3 = (bf16[1,8,16,640]{3,2,1,0:T(8,128)(2,1)S(1)}, bf16[1,8,16,640]{3,2,1,0:T(8,128)(2,1)S(1)}, u32[]{:S(2)}, u32[]{:S(2)}) collective-permute-start(bf16[1,8,16,640]{3,2,1,0:T(8,128)(2,1)S(1)} %get-tuple-element.37), channel_id=1, source_target_pairs={{0,1},{1,2},{2,3},{3,4},{4,5},{5,6},{6,7},{8,9},{9,10},{10,11},{11... | collective-permute-start | bytes 491528 | tf_op jit(solution)/shard_map/ppermute | solution.py:15
  48.6 10.5 %collective-permute-start.4 = (bf16[1,8,16,640]{3,2,1,0:T(8,128)(2,1)S(1)}, bf16[1,8,16,640]{3,2,1,0:T(8,128)(2,1)S(1)}, u32[]{:S(2)}, u32[]{:S(2)}) collective-permute-start(bf16[1,8,16,640]{3,2,1,0:T(8,128)(2,1)S(1)} %get-tuple-element.38), channel_id=1, source_target_pairs={{1,0},{2,1},{3,2},{4,3},{5,4},{6,5},{7,6},{9,8},{10,9},{11,10},{12... | collective-permute-start | bytes 491528 | tf_op jit(solution)/shard_map/ppermute | solution.py:17
  60.2 3.5 %collective-permute-start.5 = (bf16[2,8,16,640]{3,2,1,0:T(8,128)(2,1)S(1)}, bf16[2,8,16,640]{3,2,1,0:T(8,128)(2,1)S(1)}, u32[]{:S(2)}, u32[]{:S(2)}) collective-permute-start(bf16[2,8,16,640]{3,2,1,0:T(8,128)(2,1)S(1)} %fusion.29), channel_id=1, source_target_pairs={{0,8},{1,9},{2,10},{3,11},{4,12},{5,13},{6,14},{7,15},{16,24},{17,... | collective-permute-start | bytes 983048 | tf_op jit(solution)/shard_map/ppermute | solution.py:27
  67.9 15.6 %copy-start.5 = (f32[256,640]{1,0:T(8,128)S(1)}, f32[256,640]{1,0:T(8,128)}, u32[]{:S(2)}) copy-start(f32[256,640]{1,0:T(8,128)} %copy-done.4) | copy-start | bytes 1966084
  67.9 15.6 %copy-start.7 = (f32[256,640]{1,0:T(8,128)S(1)}, f32[256,640]{1,0:T(8,128)}, u32[]{:S(2)}) copy-start(f32[256,640]{1,0:T(8,128)} %copy-done.6) | copy-start | bytes 1966084
  68.7 8.5 %collective-permute-start.6 = (bf16[1,8,16,640]{3,2,1,0:T(8,128)(2,1)S(1)}, bf16[1,8,16,640]{3,2,1,0:T(8,128)(2,1)S(1)}, u32[]{:S(2)}, u32[]{:S(2)}) collective-permute-start(bf16[1,8,16,640]{3,2,1,0:T(8,128)(2,1)S(1)} %get-tuple-element.25), channel_id=1, source_target_pairs={{0,1},{1,2},{2,3},{3,4},{4,5},{5,6},{6,7},{8,9},{9,10},{10,11},{11... | collective-permute-start | bytes 491528 | tf_op jit(solution)/shard_map/ppermute | solution.py:15
  70.6 10.5 %collective-permute-start.7 = (bf16[1,8,16,640]{3,2,1,0:T(8,128)(2,1)S(1)}, bf16[1,8,16,640]{3,2,1,0:T(8,128)(2,1)S(1)}, u32[]{:S(2)}, u32[]{:S(2)}) collective-permute-start(bf16[1,8,16,640]{3,2,1,0:T(8,128)(2,1)S(1)} %get-tuple-element.26), channel_id=1, source_target_pairs={{1,0},{2,1},{3,2},{4,3},{5,4},{6,5},{7,6},{9,8},{10,9},{11,10},{12... | collective-permute-start | bytes 491528 | tf_op jit(solution)/shard_map/ppermute | solution.py:17
  82.3 3.5 %collective-permute-start.8 = (bf16[2,8,16,640]{3,2,1,0:T(8,128)(2,1)S(1)}, bf16[2,8,16,640]{3,2,1,0:T(8,128)(2,1)S(1)}, u32[]{:S(2)}, u32[]{:S(2)}) collective-permute-start(bf16[2,8,16,640]{3,2,1,0:T(8,128)(2,1)S(1)} %fusion.39), channel_id=1, source_target_pairs={{0,8},{1,9},{2,10},{3,11},{4,12},{5,13},{6,14},{7,15},{16,24},{17,... | collective-permute-start | bytes 983048 | tf_op jit(solution)/shard_map/ppermute | solution.py:27
  90.8 8.5 %collective-permute-start.9 = (bf16[1,8,16,640]{3,2,1,0:T(8,128)(2,1)S(1)}, bf16[1,8,16,640]{3,2,1,0:T(8,128)(2,1)S(1)}, u32[]{:S(2)}, u32[]{:S(2)}) collective-permute-start(bf16[1,8,16,640]{3,2,1,0:T(8,128)(2,1)S(1)} %get-tuple-element.13), channel_id=1, source_target_pairs={{0,1},{1,2},{2,3},{3,4},{4,5},{5,6},{6,7},{8,9},{9,10},{10,11},{11... | collective-permute-start | bytes 491528 | tf_op jit(solution)/shard_map/ppermute | solution.py:15
  92.7 10.5 %collective-permute-start.10 = (bf16[1,8,16,640]{3,2,1,0:T(8,128)(2,1)S(1)}, bf16[1,8,16,640]{3,2,1,0:T(8,128)(2,1)S(1)}, u32[]{:S(2)}, u32[]{:S(2)}) collective-permute-start(bf16[1,8,16,640]{3,2,1,0:T(8,128)(2,1)S(1)} %get-tuple-element.14), channel_id=1, source_target_pairs={{1,0},{2,1},{3,2},{4,3},{5,4},{6,5},{7,6},{9,8},{10,9},{11,10},{12... | collective-permute-start | bytes 491528 | tf_op jit(solution)/shard_map/ppermute | solution.py:17
where the time goes:
time: 106 us
  waiting for transfers between devices  29.1 us (27%)
  starting transfers between devices  28.8 us (27%)
  matrix products  28.1 us (27%)
  other arithmetic  14.2 us (13%)
  local copies, waits for them, and re-layouts  4.6 us (4%)
    dot_general x36, matrix products, spatial_term(): jnp.dot(window, kernels[row_tap * 3 + col_tap], preferred_element_type=jn...  22.5 us
    ppermute x4, waiting for transfers between devices, with_halo(): lax.ppermute(head, axis, [((i + 1) % count, i) for i in range(ends)])  16.1 us
    ppermute x4, starting transfers between devices, with_halo(): lax.ppermute(head, axis, [((i + 1) % count, i) for i in range(ends)])  16 us
    ppermute x4, starting transfers between devices, with_halo(): lax.ppermute(tail, axis, [(i, (i + 1) % count) for i in range(ends)])  8.88 us
    ppermute x3, waiting for transfers between devices, passed_along(): lax.ppermute(value, axis, [(source, source + steps) for source in range(i...  6.87 us
    ppermute x4, waiting for transfers between devices, with_halo(): lax.ppermute(tail, axis, [(i, (i + 1) % count) for i in range(ends)])  6.14 us
    dot_general x12, matrix products, section_local(): jnp.dot(window, temporal_kernels[frame_tap], preferred_element_type=jnp.f...  5.58 us
    convert_element_type x2, other arithmetic, dequantize(): return (weights.astype(jnp.float32) * expanded[None]).astype(jnp.bfloat16)  5.49 us
  transfers between devices with their start and end apart: 11, of which 11 were waited for; matrix products, arithmetic and copies ran while one was open for 2% of the time, Pallas kernels for 0%

commit v1 on v0

v1 whole, which is shorter than its diff:
```python
import functools

import jax
import jax.numpy as jnp
from jax import lax
from jax.experimental import pallas as pl
from jax.experimental.pallas import tpu as pltpu
from jax.sharding import PartitionSpec as P

AXES = ("groups", "segment", "seq")
VMEM = pl.BlockSpec(memory_space=pltpu.VMEM)
ANY = pl.BlockSpec(memory_space=pl.ANY)


def silu(v):
    return v / (1.0 + jnp.exp(-v))


def swap_pairs(sizes, odd, active):
    groups, segments, count = sizes

    def paired(segment, place):
        mate = place - 1 if (place + odd) % 2 else place + 1
        return mate if segment in active and 0 <= mate < count else None

    pairs = []
    for group in range(groups):
        for segment in range(segments):
            for place in range(count):
                mate = paired(segment, place)
                target = (group, segment, mate)
                if mate is None:
                    other = segment ^ 1
                    if other < segments and paired(other, place) is None:
                        target = (group, other, place)
                    elif group ^ 1 < groups:
                        target = (group ^ 1, segment, place)
                    else:
                        continue
                flat = lambda g, s, p: (g * segments + s) * count + p
                pairs.append((flat(group, segment, place), flat(*target)))
    return pairs


def spatial_kernel(slot, *refs):
    if slot == 0:
        x_ref, w_ref, s_ref = refs[:3]
        rest = refs[3:]
    else:
        first_ref, moved_ref, w_ref, s_ref = refs[:4]
        rest = refs[4:]
    mid_ref, lift_ref, even_ref, odd_ref, cols_ref = rest
    frames, height, width, channels = mid_ref.shape
    rows = frames * height * width
    blocks = s_ref.shape[0]
    block = channels // blocks
    segment = lax.axis_index("segment")
    place = lax.axis_index("seq")
    acc = jnp.zeros((rows, channels), jnp.float32)
    taps = w_ref.shape[0]
    inputs = []
    for b in range(blocks):
        part = pl.ds(b * block, block)
        if slot == 0:
            x = x_ref[:, :, :, part]
        else:
            x = jnp.where(segment == 0, first_ref[:, :, :, part], moved_ref[:, :, :, part])
        inputs.append(x)
        lifted = silu(x.astype(jnp.float32))
        edge = jnp.zeros((frames, height, 1, block), jnp.float32)
        line = jnp.zeros((frames, 1, width, block), jnp.bfloat16)
        for col in range(3):
            if col == 0:
                moved = jnp.concatenate([edge, lifted[:, :, :-1]], axis=2)
            elif col == 2:
                moved = jnp.concatenate([lifted[:, :, 1:], edge], axis=2)
            else:
                moved = lifted
            moved = moved.astype(jnp.bfloat16)
            for row in range(3):
                if row == 0:
                    window = jnp.concatenate([line, moved[:, :-1]], axis=1)
                elif row == 2:
                    window = jnp.concatenate([moved[:, 1:], line], axis=1)
                else:
                    window = moved
                cols_ref[b, :, pl.ds((row * 3 + col) * block, block)] = window.reshape(rows, block)
        weights = jnp.concatenate([w_ref[t, part, :] for t in range(taps)], axis=0)
        acc += jnp.dot(cols_ref[b], weights, preferred_element_type=jnp.float32) * s_ref[b : b + 1]
    x = jnp.concatenate(inputs, axis=3).reshape(rows, channels)
    mid = (x.astype(jnp.float32) + acc).astype(jnp.bfloat16)
    lift = silu(mid.astype(jnp.float32)).astype(jnp.bfloat16).reshape(mid_ref.shape)
    mid_ref[...] = mid.reshape(mid_ref.shape)
    lift_ref[...] = lift
    is_odd = lax.rem(place, 2) == 1
    even_ref[...] = jnp.where(is_odd, lift[0], lift[frames - 1])
    odd_ref[...] = jnp.where(is_odd, lift[frames - 1], lift[0])


def dequant_kernel(w_ref, s_ref, o_ref):
    blocks = s_ref.shape[0]
    block = w_ref.shape[1] // blocks
    for t in range(w_ref.shape[0]):
        for b in range(blocks):
            part = pl.ds(b * block, block)
            o_ref[t, part, :] = (w_ref[t, part, :].astype(jnp.float32) * s_ref[b : b + 1]).astype(
                jnp.bfloat16
            )


def temporal_kernel(slot, ticks, *refs):
    mid_ref, lift_ref, even_ref, odd_ref, w_ref = refs[:5]
    out_ref, res_ref, ext_ref, sem = refs[-4:]
    frames, height, width, channels = mid_ref.shape
    rows = frames * height * width
    segment = lax.axis_index("segment")
    place = lax.axis_index("seq")
    last = lax.axis_size("seq") - 1
    is_odd = lax.rem(place, 2) == 1
    zero = jnp.zeros((height, width, channels), jnp.bfloat16)
    even, odd = even_ref[...], odd_ref[...]
    left = jnp.where(is_odd, even, odd)
    right = jnp.where(is_odd, odd, even)
    ext_ref[0] = jnp.where(place == 0, zero, left)
    ext_ref[pl.ds(1, frames)] = lift_ref[...]
    ext_ref[frames + 1] = jnp.where(place == last, zero, right)
    acc = jnp.zeros((rows, channels), jnp.float32)
    for tap in range(w_ref.shape[0]):
        window = ext_ref[pl.ds(tap, frames)].reshape(rows, channels)
        acc += jnp.dot(window, w_ref[tap], preferred_element_type=jnp.float32)
    mid = mid_ref[...].reshape(rows, channels).astype(jnp.float32)
    res = (mid + acc.astype(jnp.bfloat16).astype(jnp.float32)).astype(jnp.bfloat16)
    res_ref[...] = res.reshape(res_ref.shape)
    tick = slot - segment
    valid = jnp.logical_and(tick >= 0, tick < ticks)

    @pl.when(valid)
    def _():
        copy = pltpu.make_async_copy(res_ref, out_ref.at[0, tick], sem)
        copy.start()
        copy.wait()


def params():
    return pltpu.CompilerParams(vmem_limit_bytes=24 << 20)


def spatial(slot, inputs, weights, scales):
    shape = inputs[0].shape
    frames, height, width, channels = shape
    rows = frames * height * width
    taps = weights.shape[0]
    blocks = scales.shape[0]
    clip = jax.ShapeDtypeStruct(shape, jnp.bfloat16)
    frame = jax.ShapeDtypeStruct(shape[1:], jnp.bfloat16)
    return pl.pallas_call(
        functools.partial(spatial_kernel, slot),
        out_shape=(clip, clip, frame, frame),
        in_specs=[VMEM] * (len(inputs) + 2),
        out_specs=[VMEM] * 4,
        scratch_shapes=[pltpu.VMEM((blocks, rows, taps * channels // blocks), jnp.bfloat16)],
        compiler_params=params(),
        cost_estimate=pl.CostEstimate(
            flops=2 * taps * rows * channels * channels,
            bytes_accessed=2 * taps * channels * channels,
            transcendentals=2 * rows * channels,
        ),
        name=f"spatial{slot}",
    )(*inputs, weights, scales)


def temporal(slot, ticks, mid, lift, even, odd, weights, out):
    shape = mid.shape
    frames, height, width, channels = shape
    rows = frames * height * width
    taps = weights.shape[0]
    operands = [mid, lift, even, odd, weights]
    aliases = {}
    if out is not None:
        aliases = {len(operands): 0}
        operands.append(out)
    return pl.pallas_call(
        functools.partial(temporal_kernel, slot, ticks),
        out_shape=(
            jax.ShapeDtypeStruct((1, ticks) + shape, jnp.bfloat16),
            jax.ShapeDtypeStruct(shape, jnp.bfloat16),
        ),
        in_specs=[VMEM] * 5 + [ANY] * len(aliases),
        out_specs=(ANY, VMEM),
        scratch_shapes=[
            pltpu.VMEM((frames + 2,) + shape[1:], jnp.bfloat16),
            pltpu.SemaphoreType.DMA,
        ],
        input_output_aliases=aliases,
        compiler_params=params(),
        cost_estimate=pl.CostEstimate(
            flops=2 * taps * rows * channels * channels,
            bytes_accessed=2 * taps * channels * channels,
            transcendentals=0,
        ),
        name=f"temporal{slot}",
    )(*operands)


def local(sizes, held, arrivals, spatial_weight, spatial_scale, temporal_weight, temporal_scale):
    groups, segments, count = sizes
    ticks = arrivals.shape[0] + 1
    slots = ticks + segments - 1
    held, weights_s, scales_s = held[0], spatial_weight[0], spatial_scale[0]
    weights_t = pl.pallas_call(
        dequant_kernel,
        out_shape=jax.ShapeDtypeStruct(temporal_weight.shape[1:], jnp.bfloat16),
        in_specs=[VMEM] * 2,
        out_specs=VMEM,
        compiler_params=params(),
        name="dequant",
    )(temporal_weight[0], temporal_scale[0])
    first = lax.axis_index("segment") == 0
    onward = [(s, (s + 1) % segments) for s in range(segments)]
    parts, results, out = [], [], None

    def finish(slot):
        nonlocal out
        mid, lift, even, odd = parts[slot]
        out, result = temporal(slot, ticks, mid, lift, even, odd, weights_t, out)
        results.append(result)

    for slot in range(slots):
        if slot == 0:
            inputs = [held]
        elif slot == 1:
            inputs = [arrivals[0], held]
        else:
            moved = lax.ppermute(results[slot - 2], "segment", onward)
            if slot - 1 < ticks - 1:
                inputs = [arrivals[slot - 1], moved]
            else:
                inputs = [moved, moved]
        mid, lift, even, odd = spatial(slot, inputs, weights_s, scales_s)
        active = [s for s in range(segments) if 0 <= slot - s < ticks]
        even = lax.ppermute(even, AXES, swap_pairs(sizes, 0, active))
        odd = lax.ppermute(odd, AXES, swap_pairs(sizes, 1, active))
        parts.append((mid, lift, even, odd))
        if slot >= 1:
            finish(slot - 1)
    finish(slots - 1)
    return out


def solution(mesh):
    sizes = tuple(mesh.shape[axis] for axis in AXES)
    in_specs = (
        P("segment", ("groups", "seq"), None, None, None),
        P(None, ("groups", "seq"), None, None, None),
        P("segment", None, None, None),
        P("segment", None, None),
        P("segment", None, None, None),
        P("segment", None, None),
    )
    out_specs = P("segment", None, ("groups", "seq"), None, None, None)
    return jax.shard_map(
        functools.partial(local, sizes),
        mesh=mesh,
        in_specs=in_specs,
        out_specs=out_specs,
        check_vma=False,
    )
```

time: 106 us -> 60.1 us (0.57)
  matrix products: 28.1 us -> 0 us
  Pallas kernels: 0 us -> 25.4 us
  waiting for transfers between devices: 29.1 us -> 12 us
  other arithmetic: 14.2 us -> 0.01 us
  starting transfers between devices: 28.8 us -> 17.2 us
    dot_general x48 -> x0, matrix products: 28.1 us -> none  [the longest x36 22.5 us: spatial_term(): jnp.dot(window, kernels[row_tap * 3 + col_tap], preferred_element_type=jn...]
    pallas_call x0 -> x11, Pallas kernels: none -> 25.4 us  [the longest x5 15.3 us: spatial(): pl.pallas_call(functools.partial(spatial_kernel, slot), out_shape=(clip,...]
    ppermute x11 -> x13, waiting for transfers between devices: 29.1 us -> 12 us  [the longest x5 10.5 us: local(): even = lax.ppermute(even, AXES, swap_pairs(sizes, 0, active))]
    convert_element_type x15 -> x0, other arithmetic: 12.6 us -> none  [the longest x2 5.49 us: dequantize(): return (weights.astype(jnp.float32) * expanded[None]).astype(jnp.bfloat16)]
    ppermute x11 -> x13, starting transfers between devices: 28.8 us -> 17.2 us  [the longest x3 10 us: local(): moved = lax.ppermute(results[slot - 2], 'segment', onward)]
    unnamed x36 -> x18, local copies, waits for them, and re-layouts: 0.81 us -> 4.81 us
    slice x8 -> x0, local copies, waits for them, and re-layouts: 2.38 us -> none  [the longest x4 2.26 us: spatial_term(): padded[:, row_tap:row_tap + height, col_tap:col_tap + width]]
    broadcast_in_dim x2 -> x0, local copies, waits for them, and re-layouts: 1.42 us -> none  [dequantize(): expanded = jnp.repeat(scales, block, axis=0)]
  transfers between devices with their start and end apart: 11 -> 13, of which waited for: 11 -> 4; matrix products, arithmetic and copies ran while one was open for 2% -> 0% of each run, Pallas kernels for 0% -> 32%
where the time goes in v1:
time: 60.1 us; the launch traced here: 59.9 us
  Pallas kernels  25.4 us (42%)
  starting transfers between devices  17.2 us (29%)
  waiting for transfers between devices  12 us (20%)
  local copies, waits for them, and re-layouts  4.89 us (8%)
    pallas_call x5, Pallas kernels, spatial(): pl.pallas_call(functools.partial(spatial_kernel, slot), out_shape=(clip,...  15.3 us
    ppermute x5, waiting for transfers between devices, local(): even = lax.ppermute(even, AXES, swap_pairs(sizes, 0, active))  10.5 us
    ppermute x3, starting transfers between devices, local(): moved = lax.ppermute(results[slot - 2], 'segment', onward)  10 us
    pallas_call x5, Pallas kernels, temporal(): pl.pallas_call(functools.partial(temporal_kernel, slot, ticks), out_shape...  9.67 us
    ppermute x5, starting transfers between devices, local(): odd = lax.ppermute(odd, AXES, swap_pairs(sizes, 1, active))  5.04 us
    unnamed x18, local copies, waits for them, and re-layouts  4.81 us
    ppermute x5, starting transfers between devices, local(): even = lax.ppermute(even, AXES, swap_pairs(sizes, 0, active))  2.14 us
    ppermute x5, waiting for transfers between devices, local(): odd = lax.ppermute(odd, AXES, swap_pairs(sizes, 1, active))  1.47 us
  transfers between devices with their start and end apart: 13, of which 4 were waited for; matrix products, arithmetic and copies ran while one was open for 0% of the time, Pallas kernels for 32%

profile of v1, /device:TPU:29, one launch (start us, length us, event | category | flops | bytes accessed | tf_op | source)
XLA Modules:
  0.0 59.9 jit_solution(5843158805380822850)
XLA Ops:
  0.0 0.7 %copy.16 = f32[1,5,640]{2,1,0:T(8,128)S(1)} copy(f32[1,5,640]{2,0,1:T(1,128)} %param.9) | data formatting | bytes 25600
  0.7 3.1 %copy-done = bf16[1,9,640,640]{3,2,1,0:T(8,128)(2,1)S(1)} copy-done((bf16[1,9,640,640]{3,2,1,0:T(8,128)(2,1)S(1)}, bf16[1,9,640,640]{3,2,1,0:T(8,128)(2,1)}, u32[]{:S(2)}) %copy-start) | copy-done | bytes 7372824
  3.8 1.0 %copy-done.2 = bf16[1,2,8,16,640]{4,3,2,1,0:T(8,128)(2,1)S(1)} copy-done((bf16[1,2,8,16,640]{4,3,2,1,0:T(8,128)(2,1)S(1)}, bf16[1,2,8,16,640]{4,3,2,1,0:T(8,128)(2,1)}, u32[]{:S(2)}) %copy-start.2) | copy-done | bytes 327704
  4.8 2.9 %spatial0.1 = (bf16[2,8,16,640]{3,2,1,0:T(8,128)(2,1)S(1)}, bf16[2,8,16,640]{3,2,1,0:T(8,128)(2,1)S(1)}, bf16[8,16,640]{2,1,0:T(8,128)(2,1)S(1)}, bf16[8,16,640]{2,1,0:T(8,128)(2,1)S(1)}) custom-call(bf16[2,8,16,640]{3,2,1,0:T(8,128)(2,1)S(1)} %bitcast.23, bf16[9,640,640]{2,1,0:T(8,128)(2,1)S(1)} %bitcast.15, f32[5,640]{1,0:T(8,128)S(1)} %bitcast.25), custom_call_target="tpu_custom_call" | custom-call | flops 1887436800 | bytes 7372800 | tf_op jit(solution)/shard_map/spatial0/pallas_call | solution.py:156
  7.7 0.3 collective-permute-start
  8.0 1.2 %collective-permute-start.1 = (bf16[8,16,640]{2,1,0:T(8,128)(2,1)S(1)}, bf16[8,16,640]{2,1,0:T(8,128)(2,1)S(1)}, u32[]{:S(2)}, u32[]{:S(2)}) collective-permute-start(bf16[8,16,640]{2,1,0:T(8,128)(2,1)S(1)} %get-tuple-element.36), channel_id=1, source_target_pairs={{0,8},{1,2},{2,1},{3,4},{4,3},{5,6},{6,5},{7,15},{8,0},{9,25},{10,... | collective-permute-start | bytes 491528 | tf_op jit(solution)/shard_map/ppermute | solution.py:242
  9.2 0.0 copy-done.5
  9.2 0.0 copy-done.1
  9.2 0.0 slice-start.1
  9.3 0.4 dequant.1.refs_4_
  9.7 2.5 %collective-permute-done.refs_2_ = bf16[8,16,640]{2,1,0:T(8,128)(2,1)S(1)} collective-permute-done((bf16[8,16,640]{2,1,0:T(8,128)(2,1)S(1)}, bf16[8,16,640]{2,1,0:T(8,128)(2,1)S(1)}, u32[]{:S(2)}, u32[]{:S(2)}) %collective-permute-start) | collective-permute-done | bytes 163872 | tf_op jit(solution)/shard_map/ppermute | solution.py:241
  12.2 1.5 %collective-permute-done.1.refs_3_ = bf16[8,16,640]{2,1,0:T(8,128)(2,1)S(1)} collective-permute-done((bf16[8,16,640]{2,1,0:T(8,128)(2,1)S(1)}, bf16[8,16,640]{2,1,0:T(8,128)(2,1)S(1)}, u32[]{:S(2)}, u32[]{:S(2)}) %collective-permute-start.1) | collective-permute-done | bytes 163872 | tf_op jit(solution)/shard_map/ppermute | solution.py:242
  13.7 1.1 %temporal0.1 = (bf16[1,4,2,8,16,640]{5,4,3,2,1,0:T(8,128)(2,1)}, bf16[2,8,16,640]{3,2,1,0:T(8,128)(2,1)S(1)}) custom-call(bf16[2,8,16,640]{3,2,1,0:T(8,128)(2,1)S(1)} %get-tuple-element.33.refs_0_, bf16[2,8,16,640]{3,2,1,0:T(8,128)(2,1)S(1)} %get-tuple-element.34.refs_1_, bf16[8,16,640]{2,1,0:T(8,128)(2,1)S(1)} %collective-permute-done.refs_2_, ...), custom_call_target="tpu_custom_call" | custom-call | flops 629145600 | bytes 2457600 | tf_op jit(solution)/shard_map/temporal0/pallas_call | solution.py:182
  14.8 0.0 copy-start.3
  14.8 3.2 %collective-permute-start.2 = (bf16[2,8,16,640]{3,2,1,0:T(8,128)(2,1)S(1)}, bf16[2,8,16,640]{3,2,1,0:T(8,128)(2,1)S(1)}, u32[]{:S(2)}, u32[]{:S(2)}) collective-permute-start(bf16[2,8,16,640]{3,2,1,0:T(8,128)(2,1)S(1)} %get-tuple-element.37), channel_id=1, source_target_pairs={{0,8},{8,0},{1,9},{9,1},{2,10},{10,2},{3,11},{11,3},{4,12},{12,4},... | collective-permute-start | bytes 983048 | tf_op jit(solution)/shard_map/ppermute | solution.py:234
  18.0 0.1 slice_bitcast_fusion
  18.1 0.0 slice-done
  18.1 0.0 slice-done.1
  18.2 0.0 copy-done.3
  18.2 3.1 %spatial1.1 = (bf16[2,8,16,640]{3,2,1,0:T(8,128)(2,1)S(1)}, bf16[2,8,16,640]{3,2,1,0:T(8,128)(2,1)S(1)}, bf16[8,16,640]{2,1,0:T(8,128)(2,1)S(1)}, bf16[8,16,640]{2,1,0:T(8,128)(2,1)S(1)}) custom-call(bf16[2,8,16,640]{3,2,1,0:T(8,128)(2,1)S(1)} %get-tuple-element.63.refs_0_, bf16[2,8,16,640]{3,2,1,0:T(8,128)(2,1)S(1)} %bitcast.24, ...), custom_call_target="tpu_custom_call" | custom-call | flops 1887436800 | bytes 7372800 | tf_op jit(solution)/shard_map/spatial1/pallas_call | solution.py:156
  21.2 0.1 collective-permute-start.5
  21.3 1.3 %collective-permute-start.6 = (bf16[8,16,640]{2,1,0:T(8,128)(2,1)S(1)}, bf16[8,16,640]{2,1,0:T(8,128)(2,1)S(1)}, u32[]{:S(2)}, u32[]{:S(2)}) collective-permute-start(bf16[8,16,640]{2,1,0:T(8,128)(2,1)S(1)} %get-tuple-element.45), channel_id=1, source_target_pairs={{0,8},{1,2},{2,1},{3,4},{4,3},{5,6},{6,5},{7,15},{8,0},{9,10},{10,... | collective-permute-start | bytes 491528 | tf_op jit(solution)/shard_map/ppermute | solution.py:242
  22.7 0.0 collective-permute-done.2.refs_1_
  22.7 3.1 %spatial2.1 = (bf16[2,8,16,640]{3,2,1,0:T(8,128)(2,1)S(1)}, bf16[2,8,16,640]{3,2,1,0:T(8,128)(2,1)S(1)}, bf16[8,16,640]{2,1,0:T(8,128)(2,1)S(1)}, bf16[8,16,640]{2,1,0:T(8,128)(2,1)S(1)}) custom-call(bf16[2,8,16,640]{3,2,1,0:T(8,128)(2,1)S(1)} %get-tuple-element.62.refs_0_, bf16[2,8,16,640]{3,2,1,0:T(8,128)(2,1)S(1)} %collective-permute-done.2.refs_1_, ...), custom_call_target="tpu_custom_call" | custom-call | flops 1887436800 | bytes 7372800 | tf_op jit(solution)/shard_map/spatial2/pallas_call | solution.py:156
  25.7 1.2 %collective-permute-start.3 = (bf16[8,16,640]{2,1,0:T(8,128)(2,1)S(1)}, bf16[8,16,640]{2,1,0:T(8,128)(2,1)S(1)}, u32[]{:S(2)}, u32[]{:S(2)}) collective-permute-start(bf16[8,16,640]{2,1,0:T(8,128)(2,1)S(1)} %get-tuple-element.40), channel_id=1, source_target_pairs={{0,1},{1,0},{2,3},{3,2},{4,5},{5,4},{6,7},{7,6},{8,9},{9,8},{10,11... | collective-permute-start | bytes 491528 | tf_op jit(solution)/shard_map/ppermute | solution.py:241
  27.0 0.2 collective-permute-start.4
  27.1 2.8 %collective-permute-done.5.refs_2_ = bf16[8,16,640]{2,1,0:T(8,128)(2,1)S(1)} collective-permute-done((bf16[8,16,640]{2,1,0:T(8,128)(2,1)S(1)}, bf16[8,16,640]{2,1,0:T(8,128)(2,1)S(1)}, u32[]{:S(2)}, u32[]{:S(2)}) %collective-permute-start.5) | collective-permute-done | bytes 163872 | tf_op jit(solution)/shard_map/ppermute | solution.py:241
  30.0 0.0 collective-permute-done.6.refs_3_
  30.0 1.8 %temporal1.1 = (bf16[1,4,2,8,16,640]{5,4,3,2,1,0:T(8,128)(2,1)}, bf16[2,8,16,640]{3,2,1,0:T(8,128)(2,1)S(1)}) custom-call(bf16[2,8,16,640]{3,2,1,0:T(8,128)(2,1)S(1)} %get-tuple-element.42.refs_0_, bf16[2,8,16,640]{3,2,1,0:T(8,128)(2,1)S(1)} %get-tuple-element.43.refs_1_, ...), custom_call_target="tpu_custom_call", output_to_operand_aliasing={{0}: (5, {})} | custom-call | flops 629145600 | bytes 2457600 | tf_op jit(solution)/shard_map/temporal1/pallas_call | solution.py:182
  31.7 6.1 %collective-permute-start.10 = (bf16[2,8,16,640]{3,2,1,0:T(8,128)(2,1)S(1)}, bf16[2,8,16,640]{3,2,1,0:T(8,128)(2,1)S(1)}, u32[]{:S(2)}, u32[]{:S(2)}) collective-permute-start(bf16[2,8,16,640]{3,2,1,0:T(8,128)(2,1)S(1)} %get-tuple-element.53), channel_id=1, source_target_pairs={{0,8},{8,0},{1,9},{9,1},{2,10},{10,2},{3,11},{11,3},{4,12},{12,4},... | collective-permute-start | bytes 983048 | tf_op jit(solution)/shard_map/ppermute | solution.py:234
  37.9 0.0 collective-permute-done.3.refs_2_
  37.9 0.0 collective-permute-done.4.refs_3_
  37.9 1.8 %temporal2.1 = (bf16[1,4,2,8,16,640]{5,4,3,2,1,0:T(8,128)(2,1)}, bf16[2,8,16,640]{3,2,1,0:T(8,128)(2,1)S(1)}) custom-call(bf16[2,8,16,640]{3,2,1,0:T(8,128)(2,1)S(1)} %get-tuple-element.38.refs_0_, bf16[2,8,16,640]{3,2,1,0:T(8,128)(2,1)S(1)} %get-tuple-element.39.refs_1_, ...), custom_call_target="tpu_custom_call", output_to_operand_aliasing={{0}: (5, {})} | custom-call | flops 629145600 | bytes 2457600 | tf_op jit(solution)/shard_map/temporal2/pallas_call | solution.py:182
  39.7 0.6 %collective-permute-start.7 = (bf16[2,8,16,640]{3,2,1,0:T(8,128)(2,1)S(1)}, bf16[2,8,16,640]{3,2,1,0:T(8,128)(2,1)S(1)}, u32[]{:S(2)}, u32[]{:S(2)}) collective-permute-start(bf16[2,8,16,640]{3,2,1,0:T(8,128)(2,1)S(1)} %get-tuple-element.48), channel_id=1, source_target_pairs={{0,8},{8,0},{1,9},{9,1},{2,10},{10,2},{3,11},{11,3},{4,12},{12,4},... | collective-permute-start | bytes 983048 | tf_op jit(solution)/shard_map/ppermute | solution.py:234
  40.3 0.0 collective-permute-done.10.refs_1_
  40.3 3.2 %spatial3.1 = (bf16[2,8,16,640]{3,2,1,0:T(8,128)(2,1)S(1)}, bf16[2,8,16,640]{3,2,1,0:T(8,128)(2,1)S(1)}, bf16[8,16,640]{2,1,0:T(8,128)(2,1)S(1)}, bf16[8,16,640]{2,1,0:T(8,128)(2,1)S(1)}) custom-call(bf16[2,8,16,640]{3,2,1,0:T(8,128)(2,1)S(1)} %get-tuple-element.61.refs_0_, bf16[2,8,16,640]{3,2,1,0:T(8,128)(2,1)S(1)} %collective-permute-done.10.refs_1_, ...), custom_call_target="tpu_custom_call" | custom-call | flops 1887436800 | bytes 7372800 | tf_op jit(solution)/shard_map/spatial3/pallas_call | solution.py:156
  43.6 0.1 collective-permute-start.11
  43.6 1.3 %collective-permute-start.12 = (bf16[8,16,640]{2,1,0:T(8,128)(2,1)S(1)}, bf16[8,16,640]{2,1,0:T(8,128)(2,1)S(1)}, u32[]{:S(2)}, u32[]{:S(2)}) collective-permute-start(bf16[8,16,640]{2,1,0:T(8,128)(2,1)S(1)} %get-tuple-element.57), channel_id=1, source_target_pairs={{0,8},{1,2},{2,1},{3,4},{4,3},{5,6},{6,5},{7,15},{8,0},{9,10},{10,... | collective-permute-start | bytes 491528 | tf_op jit(solution)/shard_map/ppermute | solution.py:242
  45.0 0.0 collective-permute-done.7.refs_0_.refs_1_
  45.0 3.1 %spatial4.1 = (bf16[2,8,16,640]{3,2,1,0:T(8,128)(2,1)S(1)}, bf16[2,8,16,640]{3,2,1,0:T(8,128)(2,1)S(1)}, bf16[8,16,640]{2,1,0:T(8,128)(2,1)S(1)}, bf16[8,16,640]{2,1,0:T(8,128)(2,1)S(1)}) custom-call(bf16[2,8,16,640]{3,2,1,0:T(8,128)(2,1)S(1)} %collective-permute-done.7.refs_0_.refs_1_, bf16[2,8,16,640]{3,2,1,0:T(8,128)(2,1)S(1)} %collective-permute-done.7.refs_0_.refs_1_, ...), custom_call_target="tpu_custom_call" | custom-call | flops 1887436800 | bytes 7372800 | tf_op jit(solution)/shard_map/spatial4/pallas_call | solution.py:156
  48.1 0.5 collective-permute-start.8
  48.5 0.9 %collective-permute-start.9 = (bf16[8,16,640]{2,1,0:T(8,128)(2,1)S(1)}, bf16[8,16,640]{2,1,0:T(8,128)(2,1)S(1)}, u32[]{:S(2)}, u32[]{:S(2)}) collective-permute-start(bf16[8,16,640]{2,1,0:T(8,128)(2,1)S(1)} %get-tuple-element.52), channel_id=1, source_target_pairs={{0,8},{1,17},{2,18},{3,19},{4,20},{5,21},{6,22},{7,15},{8,0},{9,10... | collective-permute-start | bytes 491528 | tf_op jit(solution)/shard_map/ppermute | solution.py:242
  49.5 5.2 %collective-permute-done.11.refs_2_ = bf16[8,16,640]{2,1,0:T(8,128)(2,1)S(1)} collective-permute-done((bf16[8,16,640]{2,1,0:T(8,128)(2,1)S(1)}, bf16[8,16,640]{2,1,0:T(8,128)(2,1)S(1)}, u32[]{:S(2)}, u32[]{:S(2)}) %collective-permute-start.11) | collective-permute-done | bytes 163872 | tf_op jit(solution)/shard_map/ppermute | solution.py:241
  54.6 0.0 collective-permute-done.12.refs_3_
  54.6 2.5 %temporal3.1 = (bf16[1,4,2,8,16,640]{5,4,3,2,1,0:T(8,128)(2,1)}, bf16[2,8,16,640]{3,2,1,0:T(8,128)(2,1)}) custom-call(bf16[2,8,16,640]{3,2,1,0:T(8,128)(2,1)S(1)} %get-tuple-element.54.refs_0_, bf16[2,8,16,640]{3,2,1,0:T(8,128)(2,1)S(1)} %get-tuple-element.55.refs_1_, ...), custom_call_target="tpu_custom_call", output_to_operand_aliasing={{0}: (5, {})} | custom-call | flops 629145600 | bytes 2457600 | tf_op jit(solution)/shard_map/temporal3/pallas_call | solution.py:182
  57.2 0.0 collective-permute-done.8.refs_2_
  57.2 0.0 collective-permute-done.9.refs_3_
  57.2 2.5 %temporal4.1 = (bf16[1,4,2,8,16,640]{5,4,3,2,1,0:T(8,128)(2,1)}, bf16[2,8,16,640]{3,2,1,0:T(8,128)(2,1)}) custom-call(bf16[2,8,16,640]{3,2,1,0:T(8,128)(2,1)S(1)} %get-tuple-element.49.refs_0_, bf16[2,8,16,640]{3,2,1,0:T(8,128)(2,1)S(1)} %get-tuple-element.50.refs_1_, ...), custom_call_target="tpu_custom_call", output_to_operand_aliasing={{0}: (5, {})} | custom-call | flops 629145600 | bytes 2457600 | tf_op jit(solution)/shard_map/temporal4/pallas_call | solution.py:182
  (9 shorter events, 0.0 us)
Async XLA Ops:
  0.7 3.1 %copy-start = (bf16[1,9,640,640]{3,2,1,0:T(8,128)(2,1)S(1)}, bf16[1,9,640,640]{3,2,1,0:T(8,128)(2,1)}, u32[]{:S(2)}) copy-start(bf16[1,9,640,640]{3,2,1,0:T(8,128)(2,1)} %param.8) | copy-start | bytes 22118404
  3.8 1.0 %copy-start.2 = (bf16[1,2,8,16,640]{4,3,2,1,0:T(8,128)(2,1)S(1)}, bf16[1,2,8,16,640]{4,3,2,1,0:T(8,128)(2,1)}, u32[]{:S(2)}) copy-start(bf16[1,2,8,16,640]{4,3,2,1,0:T(8,128)(2,1)} %param.6) | copy-start | bytes 983044
  4.8 4.5 %copy-start.5 = (f32[1,5,640]{2,0,1:T(1,128)S(1)}, f32[1,5,640]{2,0,1:T(1,128)}, u32[]{:S(2)}) copy-start(f32[1,5,640]{2,0,1:T(1,128)} %param.11) | copy-start | bytes 38404
  4.8 4.5 %copy-start.1 = (bf16[1,3,640,640]{3,2,1,0:T(8,128)(2,1)S(1)}, bf16[1,3,640,640]{3,2,1,0:T(8,128)(2,1)}, u32[]{:S(2)}) copy-start(bf16[1,3,640,640]{3,2,1,0:T(8,128)(2,1)} %param.10) | copy-start | bytes 7372804
  4.8 13.4 %slice-start = ((s8[7372800]{0:T(1024)(128)(4,1)}), s8[4194304]{0:T(1024)(128)(4,1)S(1)}, s32[]{:S(2)}) async-start(s8[7372800]{0:T(1024)(128)(4,1)} %bitcast.16), calls=%async_computation | async-start | bytes 8388608
  7.7 4.5 %collective-permute-start = (bf16[8,16,640]{2,1,0:T(8,128)(2,1)S(1)}, bf16[8,16,640]{2,1,0:T(8,128)(2,1)S(1)}, u32[]{:S(2)}, u32[]{:S(2)}) collective-permute-start(bf16[8,16,640]{2,1,0:T(8,128)(2,1)S(1)} %get-tuple-element.35), channel_id=1, source_target_pairs={{0,1},{1,0},{2,3},{3,2},{4,5},{5,4},{6,7},{7,6},{8,24},{9,25},{10,... | collective-permute-start | bytes 491528 | tf_op jit(solution)/shard_map/ppermute | solution.py:241
  8.0 5.7 %collective-permute-start.1 = (bf16[8,16,640]{2,1,0:T(8,128)(2,1)S(1)}, bf16[8,16,640]{2,1,0:T(8,128)(2,1)S(1)}, u32[]{:S(2)}, u32[]{:S(2)}) collective-permute-start(bf16[8,16,640]{2,1,0:T(8,128)(2,1)S(1)} %get-tuple-element.36), channel_id=1, source_target_pairs={{0,8},{1,2},{2,1},{3,4},{4,3},{5,6},{6,5},{7,15},{8,0},{9,25},{10,... | collective-permute-start | bytes 491528 | tf_op jit(solution)/shard_map/ppermute | solution.py:242
  9.2 8.9 %slice-start.1 = ((s8[7372800]{0:T(1024)(128)(4,1)}), s8[3178496]{0:T(1024)(128)(4,1)S(1)}, s32[]{:S(2)}) async-start(s8[7372800]{0:T(1024)(128)(4,1)} %bitcast.16), calls=%async_computation.1 | async-start | bytes 6356992
  13.7 4.4 %copy-start.4 = (bf16[3,2,8,16,640]{4,3,2,1,0:T(8,128)(2,1)S(1)}, bf16[3,2,8,16,640]{4,3,2,1,0:T(8,128)(2,1)}, u32[]{:S(2)}) copy-start(bf16[3,2,8,16,640]{4,3,2,1,0:T(8,128)(2,1)} %param.7) | copy-start | bytes 2949124
  14.8 3.4 %copy-start.3 = (bf16[1,2,8,16,640]{4,3,2,1,0:T(8,128)(2,1)S(1)}, bf16[1,2,8,16,640]{4,3,2,1,0:T(8,128)(2,1)}, u32[]{:S(2)}) copy-start(bf16[1,2,8,16,640]{4,3,2,1,0:T(8,128)(2,1)} %param.6) | copy-start | bytes 983044
  14.8 7.9 %collective-permute-start.2 = (bf16[2,8,16,640]{3,2,1,0:T(8,128)(2,1)S(1)}, bf16[2,8,16,640]{3,2,1,0:T(8,128)(2,1)S(1)}, u32[]{:S(2)}, u32[]{:S(2)}) collective-permute-start(bf16[2,8,16,640]{3,2,1,0:T(8,128)(2,1)S(1)} %get-tuple-element.37), channel_id=1, source_target_pairs={{0,8},{8,0},{1,9},{9,1},{2,10},{10,2},{3,11},{11,3},{4,12},{12,4},... | collective-permute-start | bytes 983048 | tf_op jit(solution)/shard_map/ppermute | solution.py:234
  21.2 8.7 %collective-permute-start.5 = (bf16[8,16,640]{2,1,0:T(8,128)(2,1)S(1)}, bf16[8,16,640]{2,1,0:T(8,128)(2,1)S(1)}, u32[]{:S(2)}, u32[]{:S(2)}) collective-permute-start(bf16[8,16,640]{2,1,0:T(8,128)(2,1)S(1)} %get-tuple-element.44), channel_id=1, source_target_pairs={{0,1},{1,0},{2,3},{3,2},{4,5},{5,4},{6,7},{7,6},{8,9},{9,8},{10,11... | collective-permute-start | bytes 491528 | tf_op jit(solution)/shard_map/ppermute | solution.py:241
  21.3 8.6 %collective-permute-start.6 = (bf16[8,16,640]{2,1,0:T(8,128)(2,1)S(1)}, bf16[8,16,640]{2,1,0:T(8,128)(2,1)S(1)}, u32[]{:S(2)}, u32[]{:S(2)}) collective-permute-start(bf16[8,16,640]{2,1,0:T(8,128)(2,1)S(1)} %get-tuple-element.45), channel_id=1, source_target_pairs={{0,8},{1,2},{2,1},{3,4},{4,3},{5,6},{6,5},{7,15},{8,0},{9,10},{10,... | collective-permute-start | bytes 491528 | tf_op jit(solution)/shard_map/ppermute | solution.py:242
  25.7 12.1 %collective-permute-start.3 = (bf16[8,16,640]{2,1,0:T(8,128)(2,1)S(1)}, bf16[8,16,640]{2,1,0:T(8,128)(2,1)S(1)}, u32[]{:S(2)}, u32[]{:S(2)}) collective-permute-start(bf16[8,16,640]{2,1,0:T(8,128)(2,1)S(1)} %get-tuple-element.40), channel_id=1, source_target_pairs={{0,1},{1,0},{2,3},{3,2},{4,5},{5,4},{6,7},{7,6},{8,9},{9,8},{10,11... | collective-permute-start | bytes 491528 | tf_op jit(solution)/shard_map/ppermute | solution.py:241
  27.0 10.9 %collective-permute-start.4 = (bf16[8,16,640]{2,1,0:T(8,128)(2,1)S(1)}, bf16[8,16,640]{2,1,0:T(8,128)(2,1)S(1)}, u32[]{:S(2)}, u32[]{:S(2)}) collective-permute-start(bf16[8,16,640]{2,1,0:T(8,128)(2,1)S(1)} %get-tuple-element.41), channel_id=1, source_target_pairs={{0,8},{1,2},{2,1},{3,4},{4,3},{5,6},{6,5},{7,15},{8,0},{9,10},{10,... | collective-permute-start | bytes 491528 | tf_op jit(solution)/shard_map/ppermute | solution.py:242
  31.7 8.6 %collective-permute-start.10 = (bf16[2,8,16,640]{3,2,1,0:T(8,128)(2,1)S(1)}, bf16[2,8,16,640]{3,2,1,0:T(8,128)(2,1)S(1)}, u32[]{:S(2)}, u32[]{:S(2)}) collective-permute-start(bf16[2,8,16,640]{3,2,1,0:T(8,128)(2,1)S(1)} %get-tuple-element.53), channel_id=1, source_target_pairs={{0,8},{8,0},{1,9},{9,1},{2,10},{10,2},{3,11},{11,3},{4,12},{12,4},... | collective-permute-start | bytes 983048 | tf_op jit(solution)/shard_map/ppermute | solution.py:234
  39.7 5.3 %collective-permute-start.7 = (bf16[2,8,16,640]{3,2,1,0:T(8,128)(2,1)S(1)}, bf16[2,8,16,640]{3,2,1,0:T(8,128)(2,1)S(1)}, u32[]{:S(2)}, u32[]{:S(2)}) collective-permute-start(bf16[2,8,16,640]{3,2,1,0:T(8,128)(2,1)S(1)} %get-tuple-element.48), channel_id=1, source_target_pairs={{0,8},{8,0},{1,9},{9,1},{2,10},{10,2},{3,11},{11,3},{4,12},{12,4},... | collective-permute-start | bytes 983048 | tf_op jit(solution)/shard_map/ppermute | solution.py:234
  43.6 11.1 %collective-permute-start.11 = (bf16[8,16,640]{2,1,0:T(8,128)(2,1)S(1)}, bf16[8,16,640]{2,1,0:T(8,128)(2,1)S(1)}, u32[]{:S(2)}, u32[]{:S(2)}) collective-permute-start(bf16[8,16,640]{2,1,0:T(8,128)(2,1)S(1)} %get-tuple-element.56), channel_id=1, source_target_pairs={{0,1},{1,0},{2,3},{3,2},{4,5},{5,4},{6,7},{7,6},{8,9},{9,8},{10,11... | collective-permute-start | bytes 491528 | tf_op jit(solution)/shard_map/ppermute | solution.py:241
  43.6 11.0 %collective-permute-start.12 = (bf16[8,16,640]{2,1,0:T(8,128)(2,1)S(1)}, bf16[8,16,640]{2,1,0:T(8,128)(2,1)S(1)}, u32[]{:S(2)}, u32[]{:S(2)}) collective-permute-start(bf16[8,16,640]{2,1,0:T(8,128)(2,1)S(1)} %get-tuple-element.57), channel_id=1, source_target_pairs={{0,8},{1,2},{2,1},{3,4},{4,3},{5,6},{6,5},{7,15},{8,0},{9,10},{10,... | collective-permute-start | bytes 491528 | tf_op jit(solution)/shard_map/ppermute | solution.py:242
  48.1 9.1 %collective-permute-start.8 = (bf16[8,16,640]{2,1,0:T(8,128)(2,1)S(1)}, bf16[8,16,640]{2,1,0:T(8,128)(2,1)S(1)}, u32[]{:S(2)}, u32[]{:S(2)}) collective-permute-start(bf16[8,16,640]{2,1,0:T(8,128)(2,1)S(1)} %get-tuple-element.51), channel_id=1, source_target_pairs={{0,16},{1,17},{2,18},{3,19},{4,20},{5,21},{6,22},{7,23},{8,9},{9,8... | collective-permute-start | bytes 491528 | tf_op jit(solution)/shard_map/ppermute | solution.py:241
  48.5 8.6 %collective-permute-start.9 = (bf16[8,16,640]{2,1,0:T(8,128)(2,1)S(1)}, bf16[8,16,640]{2,1,0:T(8,128)(2,1)S(1)}, u32[]{:S(2)}, u32[]{:S(2)}) collective-permute-start(bf16[8,16,640]{2,1,0:T(8,128)(2,1)S(1)} %get-tuple-element.52), channel_id=1, source_target_pairs={{0,8},{1,17},{2,18},{3,19},{4,20},{5,21},{6,22},{7,15},{8,0},{9,10... | collective-permute-start | bytes 491528 | tf_op jit(solution)/shard_map/ppermute | solution.py:242

commit v2 on v1

--- a/solution.py
+++ b/solution.py
@@ -10,6 +10,7 @@
 AXES = ("groups", "segment", "seq")
 VMEM = pl.BlockSpec(memory_space=pltpu.VMEM)
 ANY = pl.BlockSpec(memory_space=pl.ANY)
+HBM = pl.BlockSpec(memory_space=pltpu.HBM)
 
 
 def silu(v):
@@ -44,27 +45,35 @@
 
 def spatial_kernel(slot, *refs):
     if slot == 0:
-        x_ref, w_ref, s_ref = refs[:3]
-        rest = refs[3:]
+        x_ref, hbm_ref, s_ref, mid_ref, lift_ref, even_ref, odd_ref, w_ref, cols_ref, sems = refs
     else:
-        first_ref, moved_ref, w_ref, s_ref = refs[:4]
-        rest = refs[4:]
-    mid_ref, lift_ref, even_ref, odd_ref, cols_ref = rest
+        first_ref, moved_ref, w_ref, s_ref, mid_ref, lift_ref, even_ref, odd_ref, cols_ref = refs
     frames, height, width, channels = mid_ref.shape
     rows = frames * height * width
-    blocks = s_ref.shape[0]
+    blocks = cols_ref.shape[0]
     block = channels // blocks
+    taps = w_ref.shape[0]
+    copies = []
+    if slot == 0:
+        for b in range(blocks):
+            part = pl.ds(b * block, block)
+            copies.append(
+                pltpu.make_async_copy(hbm_ref.at[:, part], w_ref.at[:, part], sems.at[b])
+            )
+            copies[-1].start()
     segment = lax.axis_index("segment")
     place = lax.axis_index("seq")
+    tick = slot - 1
     acc = jnp.zeros((rows, channels), jnp.float32)
-    taps = w_ref.shape[0]
     inputs = []
     for b in range(blocks):
         part = pl.ds(b * block, block)
         if slot == 0:
             x = x_ref[:, :, :, part]
+        elif tick >= first_ref.shape[0]:
+            x = moved_ref[:, :, :, part]
         else:
-            x = jnp.where(segment == 0, first_ref[:, :, :, part], moved_ref[:, :, :, part])
+            x = jnp.where(segment == 0, first_ref[tick, :, :, :, part], moved_ref[:, :, :, part])
         inputs.append(x)
         lifted = silu(x.astype(jnp.float32))
         edge = jnp.zeros((frames, height, 1, block), jnp.float32)
@@ -85,8 +94,10 @@
                 else:
                     window = moved
                 cols_ref[b, :, pl.ds((row * 3 + col) * block, block)] = window.reshape(rows, block)
+        if copies:
+            copies[b].wait()
         weights = jnp.concatenate([w_ref[t, part, :] for t in range(taps)], axis=0)
-        acc += jnp.dot(cols_ref[b], weights, preferred_element_type=jnp.float32) * s_ref[b : b + 1]
+        acc += jnp.dot(cols_ref[b], weights, preferred_element_type=jnp.float32) * s_ref[b]
     x = jnp.concatenate(inputs, axis=3).reshape(rows, channels)
     mid = (x.astype(jnp.float32) + acc).astype(jnp.bfloat16)
     lift = silu(mid.astype(jnp.float32)).astype(jnp.bfloat16).reshape(mid_ref.shape)
@@ -100,23 +111,34 @@
 def dequant_kernel(w_ref, s_ref, o_ref):
     blocks = s_ref.shape[0]
     block = w_ref.shape[1] // blocks
-    for t in range(w_ref.shape[0]):
-        for b in range(blocks):
-            part = pl.ds(b * block, block)
-            o_ref[t, part, :] = (w_ref[t, part, :].astype(jnp.float32) * s_ref[b : b + 1]).astype(
+    for b in range(blocks):
+        part = pl.ds(b * block, block)
+        for t in range(w_ref.shape[0]):
+            o_ref[t, part, :] = (w_ref[t, part, :].astype(jnp.float32) * s_ref[b]).astype(
                 jnp.bfloat16
             )
 
 
-def temporal_kernel(slot, ticks, *refs):
+def temporal_kernel(slot, slots, ticks, *refs):
     mid_ref, lift_ref, even_ref, odd_ref, w_ref = refs[:5]
-    out_ref, res_ref, ext_ref, sem = refs[-4:]
+    out_ref, res_ref, ext_ref, sems = refs[-4:]
     frames, height, width, channels = mid_ref.shape
     rows = frames * height * width
     segment = lax.axis_index("segment")
     place = lax.axis_index("seq")
     last = lax.axis_size("seq") - 1
     is_odd = lax.rem(place, 2) == 1
+
+    def emit(source, number, act):
+        tick = number - segment
+
+        @pl.when(jnp.logical_and(tick >= 0, tick < ticks))
+        def _():
+            act(pltpu.make_async_copy(source, out_ref.at[0, tick], sems.at[number % 2]))
+
+    if slot > 0:
+        before_ref = refs[5]
+        emit(before_ref, slot - 1, lambda copy: copy.start())
     zero = jnp.zeros((height, width, channels), jnp.bfloat16)
     even, odd = even_ref[...], odd_ref[...]
     left = jnp.where(is_odd, even, odd)
@@ -131,35 +153,40 @@
     mid = mid_ref[...].reshape(rows, channels).astype(jnp.float32)
     res = (mid + acc.astype(jnp.bfloat16).astype(jnp.float32)).astype(jnp.bfloat16)
     res_ref[...] = res.reshape(res_ref.shape)
-    tick = slot - segment
-    valid = jnp.logical_and(tick >= 0, tick < ticks)
-
-    @pl.when(valid)
-    def _():
-        copy = pltpu.make_async_copy(res_ref, out_ref.at[0, tick], sem)
-        copy.start()
-        copy.wait()
-
-
-def params():
-    return pltpu.CompilerParams(vmem_limit_bytes=24 << 20)
+    if slot == slots - 1:
+        emit(res_ref, slot, lambda copy: copy.start())
+        emit(res_ref, slot, lambda copy: copy.wait())
+    if slot > 0:
+        emit(before_ref, slot - 1, lambda copy: copy.wait())
+
+
+def params(mebibytes=24):
+    return pltpu.CompilerParams(vmem_limit_bytes=mebibytes << 20)
 
 
 def spatial(slot, inputs, weights, scales):
-    shape = inputs[0].shape
+    shape = inputs[-1].shape
     frames, height, width, channels = shape
     rows = frames * height * width
     taps = weights.shape[0]
     blocks = scales.shape[0]
+    block = channels // blocks
     clip = jax.ShapeDtypeStruct(shape, jnp.bfloat16)
     frame = jax.ShapeDtypeStruct(shape[1:], jnp.bfloat16)
+    out_shape = [clip, clip, frame, frame]
+    scratch = [pltpu.VMEM((blocks, rows, taps * block), jnp.bfloat16)]
+    weight_spec = VMEM
+    if slot == 0:
+        out_shape.append(jax.ShapeDtypeStruct(weights.shape, weights.dtype))
+        scratch.append(pltpu.SemaphoreType.DMA((blocks,)))
+        weight_spec = HBM
     return pl.pallas_call(
         functools.partial(spatial_kernel, slot),
-        out_shape=(clip, clip, frame, frame),
-        in_specs=[VMEM] * (len(inputs) + 2),
-        out_specs=[VMEM] * 4,
-        scratch_shapes=[pltpu.VMEM((blocks, rows, taps * channels // blocks), jnp.bfloat16)],
-        compiler_params=params(),
+        out_shape=out_shape,
+        in_specs=[VMEM] * len(inputs) + [weight_spec, VMEM],
+        out_specs=[VMEM] * len(out_shape),
+        scratch_shapes=scratch,
+        compiler_params=params(44 if slot == 0 else 24),
         cost_estimate=pl.CostEstimate(
             flops=2 * taps * rows * channels * channels,
             bytes_accessed=2 * taps * channels * channels,
@@ -169,27 +196,32 @@
     )(*inputs, weights, scales)
 
 
-def temporal(slot, ticks, mid, lift, even, odd, weights, out):
+def temporal(slot, slots, ticks, mid, lift, even, odd, weights, before, out):
     shape = mid.shape
     frames, height, width, channels = shape
     rows = frames * height * width
     taps = weights.shape[0]
     operands = [mid, lift, even, odd, weights]
+    specs = [VMEM] * 5
     aliases = {}
-    if out is not None:
+    if slot > 0:
+        operands.append(before)
+        specs.append(VMEM)
+    if slot > 1:
         aliases = {len(operands): 0}
         operands.append(out)
+        specs.append(ANY)
     return pl.pallas_call(
-        functools.partial(temporal_kernel, slot, ticks),
+        functools.partial(temporal_kernel, slot, slots, ticks),
         out_shape=(
             jax.ShapeDtypeStruct((1, ticks) + shape, jnp.bfloat16),
             jax.ShapeDtypeStruct(shape, jnp.bfloat16),
         ),
-        in_specs=[VMEM] * 5 + [ANY] * len(aliases),
+        in_specs=specs,
         out_specs=(ANY, VMEM),
         scratch_shapes=[
             pltpu.VMEM((frames + 2,) + shape[1:], jnp.bfloat16),
-            pltpu.SemaphoreType.DMA,
+            pltpu.SemaphoreType.DMA((2,)),
         ],
         input_output_aliases=aliases,
         compiler_params=params(),
@@ -206,7 +238,8 @@
     groups, segments, count = sizes
     ticks = arrivals.shape[0] + 1
     slots = ticks + segments - 1
-    held, weights_s, scales_s = held[0], spatial_weight[0], spatial_scale[0]
+    held, weights_s = held[0], spatial_weight[0]
+    scales_s = jnp.swapaxes(spatial_scale, 0, 1)
     weights_t = pl.pallas_call(
         dequant_kernel,
         out_shape=jax.ShapeDtypeStruct(temporal_weight.shape[1:], jnp.bfloat16),
@@ -214,35 +247,37 @@
         out_specs=VMEM,
         compiler_params=params(),
         name="dequant",
-    )(temporal_weight[0], temporal_scale[0])
-    first = lax.axis_index("segment") == 0
+    )(temporal_weight[0], jnp.swapaxes(temporal_scale, 0, 1))
     onward = [(s, (s + 1) % segments) for s in range(segments)]
     parts, results, out = [], [], None
 
-    def finish(slot):
+    def finish(slot, after=None):
         nonlocal out
         mid, lift, even, odd = parts[slot]
-        out, result = temporal(slot, ticks, mid, lift, even, odd, weights_t, out)
+        if after is not None:
+            mid, _ = lax.optimization_barrier((mid, after))
+        before = results[-1] if results else None
+        out, result = temporal(slot, slots, ticks, mid, lift, even, odd, weights_t, before, out)
         results.append(result)
 
     for slot in range(slots):
         if slot == 0:
             inputs = [held]
         elif slot == 1:
-            inputs = [arrivals[0], held]
+            inputs = [arrivals, held]
         else:
             moved = lax.ppermute(results[slot - 2], "segment", onward)
-            if slot - 1 < ticks - 1:
-                inputs = [arrivals[slot - 1], moved]
-            else:
-                inputs = [moved, moved]
-        mid, lift, even, odd = spatial(slot, inputs, weights_s, scales_s)
+            inputs = [arrivals, moved]
+        made = spatial(slot, inputs, weights_s, scales_s)
+        mid, lift, even, odd = made[:4]
+        if slot == 0:
+            weights_s = made[4]
         active = [s for s in range(segments) if 0 <= slot - s < ticks]
-        even = lax.ppermute(even, AXES, swap_pairs(sizes, 0, active))
-        odd = lax.ppermute(odd, AXES, swap_pairs(sizes, 1, active))
-        parts.append((mid, lift, even, odd))
+        even_in = lax.ppermute(even, AXES, swap_pairs(sizes, 0, active))
+        odd_in = lax.ppermute(odd, AXES, swap_pairs(sizes, 1, active))
+        parts.append((mid, lift, even_in, odd_in))
         if slot >= 1:
-            finish(slot - 1)
+            finish(slot - 1, even)
     finish(slots - 1)
     return out
 

time: 60.1 us -> 55.2 us (0.918)
  starting transfers between devices: 17.2 us -> 11.2 us
  waiting for transfers between devices: 12 us -> 16.9 us
  local copies, waits for them, and re-layouts: 4.89 us -> 1.69 us
    ppermute x3, starting transfers between devices: 10 us -> 4.53 us  [local(): moved = lax.ppermute(results[slot - 2], 'segment', onward)]
    ppermute x10, waiting for transfers between devices: 12 us -> 16.9 us  [the longest x5 10.4 us: local(): even_in = lax.ppermute(even, AXES, swap_pairs(sizes, 0, active))]
    unnamed x18 -> x12, local copies, waits for them, and re-layouts: 4.81 us -> 1.69 us
  transfers between devices with their start and end apart: 13 -> 13, of which waited for: 4 -> 8; matrix products, arithmetic and copies ran while one was open for 0% -> 0% of each run, Pallas kernels for 32% -> 25%
where the time goes in v2:
time: 55.2 us; the launch traced here: 55 us
  Pallas kernels  24.9 us (45%)
  waiting for transfers between devices  16.9 us (31%)
  starting transfers between devices  11.2 us (20%)
  local copies, waits for them, and re-layouts  1.69 us (3%)
    pallas_call x5, Pallas kernels, spatial(): pl.pallas_call(functools.partial(spatial_kernel, slot), out_shape=out_sha...  17.2 us
    ppermute x5, waiting for transfers between devices, local(): even_in = lax.ppermute(even, AXES, swap_pairs(sizes, 0, active))  10.4 us
    pallas_call x5, Pallas kernels, temporal(): pl.pallas_call(functools.partial(temporal_kernel, slot, slots, ticks), ou...  7.24 us
    ppermute x5, waiting for transfers between devices, local(): odd_in = lax.ppermute(odd, AXES, swap_pairs(sizes, 1, active))  6.54 us
    ppermute x5, starting transfers between devices, local(): odd_in = lax.ppermute(odd, AXES, swap_pairs(sizes, 1, active))  6.36 us
    ppermute x3, starting transfers between devices, local(): moved = lax.ppermute(results[slot - 2], 'segment', onward)  4.53 us
    unnamed x12, local copies, waits for them, and re-layouts  1.69 us
  transfers between devices with their start and end apart: 13, of which 8 were waited for; matrix products, arithmetic and copies ran while one was open for 0% of the time, Pallas kernels for 25%

profile of v2, /device:TPU:29, one launch (start us, length us, event | category | flops | bytes accessed | tf_op | source)
XLA Modules:
  0.0 55.0 jit_solution(8029481232343332676)
XLA Ops:
  0.0 0.0 copy-start.2
  0.0 1.0 %copy-done.2 = bf16[1,2,8,16,640]{4,3,2,1,0:T(8,128)(2,1)S(1)} copy-done((bf16[1,2,8,16,640]{4,3,2,1,0:T(8,128)(2,1)S(1)}, bf16[1,2,8,16,640]{4,3,2,1,0:T(8,128)(2,1)}, u32[]{:S(2)}) %copy-start.2) | copy-done | bytes 327704
  1.0 0.0 copy-start.3
  1.0 0.7 %copy-done.3 = f32[1,5,640]{2,0,1:T(1,128)S(1)} copy-done((f32[1,5,640]{2,0,1:T(1,128)S(1)}, f32[1,5,640]{2,0,1:T(1,128)}, u32[]{:S(2)}) %copy-start.3) | copy-done | bytes 12824
  1.7 0.0 copy-start
  1.7 0.0 copy-start.4
  1.7 5.3 %spatial0.1 = (bf16[2,8,16,640]{3,2,1,0:T(8,128)(2,1)S(1)}, bf16[2,8,16,640]{3,2,1,0:T(8,128)(2,1)S(1)}, bf16[8,16,640]{2,1,0:T(8,128)(2,1)S(1)}, bf16[8,16,640]...) custom-call(bf16[2,8,16,640]{3,2,1,0:T(8,128)(2,1)S(1)} %bitcast.6, bf16[9,640,640]{2,1,0:T(8,128)(2,1)} %bitcast.14, ...), custom_call_target="tpu_custom_call" | custom-call | flops 1887436800 | bytes 7372800 | tf_op jit(solution)/shard_map/spatial0/pallas_call | solution.py:183
  7.0 0.3 collective-permute-start
  7.3 1.2 %collective-permute-start.1 = (bf16[8,16,640]{2,1,0:T(8,128)(2,1)S(1)}, bf16[8,16,640]{2,1,0:T(8,128)(2,1)S(1)}, u32[]{:S(2)}, u32[]{:S(2)}) collective-permute-start(bf16[8,16,640]{2,1,0:T(8,128)(2,1)S(1)} %get-tuple-element.44), channel_id=1, source_target_pairs={{0,8},{1,2},{2,1},{3,4},{4,3},{5,6},{6,5},{7,15},{8,0},{9,25},{10,... | collective-permute-start | bytes 491528 | tf_op jit(solution)/shard_map/ppermute | solution.py:277
  8.5 0.0 copy-done
  8.5 0.0 copy-done.4
  8.5 0.0 copy-start.1
  8.5 2.9 %spatial1.1 = (bf16[2,8,16,640]{3,2,1,0:T(8,128)(2,1)S(1)}, bf16[2,8,16,640]{3,2,1,0:T(8,128)(2,1)S(1)}, bf16[8,16,640]{2,1,0:T(8,128)(2,1)S(1)}, bf16[8,16,640]{2,1,0:T(8,128)(2,1)S(1)}) custom-call(bf16[3,2,8,16,640]{4,3,2,1,0:T(8,128)(2,1)S(1)} %copy-done, bf16[2,8,16,640]{3,2,1,0:T(8,128)(2,1)S(1)} %bitcast.7, ...), custom_call_target="tpu_custom_call" | custom-call | flops 1887436800 | bytes 7372800 | tf_op jit(solution)/shard_map/spatial1/pallas_call | solution.py:183
  11.5 0.0 copy-done.1
  11.5 0.0 copy-done.5
  11.5 0.4 dequant.1.refs_4_
  11.9 0.0 collective-permute-done.refs_2_
  11.9 1.0 %collective-permute-done.1.refs_3_ = bf16[8,16,640]{2,1,0:T(8,128)(2,1)S(1)} collective-permute-done((bf16[8,16,640]{2,1,0:T(8,128)(2,1)S(1)}, bf16[8,16,640]{2,1,0:T(8,128)(2,1)S(1)}, u32[]{:S(2)}, u32[]{:S(2)}) %collective-permute-start.1) | collective-permute-done | bytes 163872 | tf_op jit(solution)/shard_map/ppermute | solution.py:277
  13.0 1.1 %temporal0.1 = (bf16[1,4,2,8,16,640]{5,4,3,2,1,0:T(8,128)(2,1)}, bf16[2,8,16,640]{3,2,1,0:T(8,128)(2,1)S(1)}) custom-call(bf16[2,8,16,640]{3,2,1,0:T(8,128)(2,1)S(1)} %get-tuple-element.41.refs_0_, bf16[2,8,16,640]{3,2,1,0:T(8,128)(2,1)S(1)} %get-tuple-element.42.refs_1_, bf16[8,16,640]{2,1,0:T(8,128)(2,1)S(1)} %collective-permute-done.refs_2_, ...), custom_call_target="tpu_custom_call" | custom-call | flops 629145600 | bytes 2457600 | tf_op jit(solution)/shard_map/temporal0/pallas_call | solution.py:214
  14.1 2.5 %collective-permute-start.2 = (bf16[2,8,16,640]{3,2,1,0:T(8,128)(2,1)S(1)}, bf16[2,8,16,640]{3,2,1,0:T(8,128)(2,1)S(1)}, u32[]{:S(2)}, u32[]{:S(2)}) collective-permute-start(bf16[2,8,16,640]{3,2,1,0:T(8,128)(2,1)S(1)} %get-tuple-element.45.refs_5_), channel_id=1, source_target_pairs={{0,8},{8,0},{1,9},{9,1},{2,10},{10,2},{3,11},{11,3},{4,12},{12,4},... | collective-permute-start | bytes 983048 | tf_op jit(solution)/shard_map/ppermute | solution.py:269
  16.6 0.0 collective-permute-start.3
  16.6 1.3 %collective-permute-start.4 = (bf16[8,16,640]{2,1,0:T(8,128)(2,1)S(1)}, bf16[8,16,640]{2,1,0:T(8,128)(2,1)S(1)}, u32[]{:S(2)}, u32[]{:S(2)}) collective-permute-start(bf16[8,16,640]{2,1,0:T(8,128)(2,1)S(1)} %get-tuple-element.51), channel_id=1, source_target_pairs={{0,8},{1,2},{2,1},{3,4},{4,3},{5,6},{6,5},{7,15},{8,0},{9,10},{10,... | collective-permute-start | bytes 491528 | tf_op jit(solution)/shard_map/ppermute | solution.py:277
  17.9 0.0 collective-permute-done.2.refs_1_
  17.9 2.9 %spatial2.1 = (bf16[2,8,16,640]{3,2,1,0:T(8,128)(2,1)S(1)}, bf16[2,8,16,640]{3,2,1,0:T(8,128)(2,1)S(1)}, bf16[8,16,640]{2,1,0:T(8,128)(2,1)S(1)}, bf16[8,16,640]{2,1,0:T(8,128)(2,1)S(1)}) custom-call(bf16[3,2,8,16,640]{4,3,2,1,0:T(8,128)(2,1)S(1)} %copy-done, bf16[2,8,16,640]{3,2,1,0:T(8,128)(2,1)S(1)} %collective-permute-done.2.refs_1_, ...), custom_call_target="tpu_custom_call" | custom-call | flops 1887436800 | bytes 7372800 | tf_op jit(solution)/shard_map/spatial2/pallas_call | solution.py:183
  20.9 2.2 %collective-permute-done.4.refs_3_ = bf16[8,16,640]{2,1,0:T(8,128)(2,1)S(1)} collective-permute-done((bf16[8,16,640]{2,1,0:T(8,128)(2,1)S(1)}, bf16[8,16,640]{2,1,0:T(8,128)(2,1)S(1)}, u32[]{:S(2)}, u32[]{:S(2)}) %collective-permute-start.4) | collective-permute-done | bytes 163872 | tf_op jit(solution)/shard_map/ppermute | solution.py:277
  23.1 2.6 %collective-permute-done.3.refs_2_ = bf16[8,16,640]{2,1,0:T(8,128)(2,1)S(1)} collective-permute-done((bf16[8,16,640]{2,1,0:T(8,128)(2,1)S(1)}, bf16[8,16,640]{2,1,0:T(8,128)(2,1)S(1)}, u32[]{:S(2)}, u32[]{:S(2)}) %collective-permute-start.3) | collective-permute-done | bytes 163872 | tf_op jit(solution)/shard_map/ppermute | solution.py:276
  25.8 1.1 %temporal1.1 = (bf16[1,4,2,8,16,640]{5,4,3,2,1,0:T(8,128)(2,1)}, bf16[2,8,16,640]{3,2,1,0:T(8,128)(2,1)S(1)}) custom-call(bf16[2,8,16,640]{3,2,1,0:T(8,128)(2,1)S(1)} %get-tuple-element.49.refs_0_, bf16[2,8,16,640]{3,2,1,0:T(8,128)(2,1)S(1)} %get-tuple-element.50.refs_1_, bf16[8,16,640]{2,1,0:T(8,128)(2,1)S(1)} %collective-permute-done.3.refs_2_, ...), custom_call_target="tpu_custom_call" | custom-call | flops 629145600 | bytes 2457600 | tf_op jit(solution)/shard_map/temporal1/pallas_call | solution.py:214
  26.9 1.0 %collective-permute-start.5 = (bf16[2,8,16,640]{3,2,1,0:T(8,128)(2,1)S(1)}, bf16[2,8,16,640]{3,2,1,0:T(8,128)(2,1)S(1)}, u32[]{:S(2)}, u32[]{:S(2)}) collective-permute-start(bf16[2,8,16,640]{3,2,1,0:T(8,128)(2,1)S(1)} %get-tuple-element.52.refs_5_), channel_id=1, source_target_pairs={{0,8},{8,0},{1,9},{9,1},{2,10},{10,2},{3,11},{11,3},{4,12},{12,4},... | collective-permute-start | bytes 983048 | tf_op jit(solution)/shard_map/ppermute | solution.py:269
  27.9 0.0 collective-permute-start.6
  27.9 1.3 %collective-permute-start.7 = (bf16[8,16,640]{2,1,0:T(8,128)(2,1)S(1)}, bf16[8,16,640]{2,1,0:T(8,128)(2,1)S(1)}, u32[]{:S(2)}, u32[]{:S(2)}) collective-permute-start(bf16[8,16,640]{2,1,0:T(8,128)(2,1)S(1)} %get-tuple-element.56), channel_id=1, source_target_pairs={{0,8},{1,2},{2,1},{3,4},{4,3},{5,6},{6,5},{7,15},{8,0},{9,10},{10,... | collective-permute-start | bytes 491528 | tf_op jit(solution)/shard_map/ppermute | solution.py:277
  29.2 0.0 collective-permute-done.5.refs_1_
  29.2 3.1 %spatial3.1 = (bf16[2,8,16,640]{3,2,1,0:T(8,128)(2,1)S(1)}, bf16[2,8,16,640]{3,2,1,0:T(8,128)(2,1)S(1)}, bf16[8,16,640]{2,1,0:T(8,128)(2,1)S(1)}, bf16[8,16,640]{2,1,0:T(8,128)(2,1)S(1)}) custom-call(bf16[3,2,8,16,640]{4,3,2,1,0:T(8,128)(2,1)S(1)} %copy-done, bf16[2,8,16,640]{3,2,1,0:T(8,128)(2,1)S(1)} %collective-permute-done.5.refs_1_, ...), custom_call_target="tpu_custom_call" | custom-call | flops 1887436800 | bytes 7372800 | tf_op jit(solution)/shard_map/spatial3/pallas_call | solution.py:183
  32.4 2.1 %collective-permute-done.7.refs_3_ = bf16[8,16,640]{2,1,0:T(8,128)(2,1)S(1)} collective-permute-done((bf16[8,16,640]{2,1,0:T(8,128)(2,1)S(1)}, bf16[8,16,640]{2,1,0:T(8,128)(2,1)S(1)}, u32[]{:S(2)}, u32[]{:S(2)}) %collective-permute-start.7) | collective-permute-done | bytes 163872 | tf_op jit(solution)/shard_map/ppermute | solution.py:277
  34.4 2.6 %collective-permute-done.6.refs_2_ = bf16[8,16,640]{2,1,0:T(8,128)(2,1)S(1)} collective-permute-done((bf16[8,16,640]{2,1,0:T(8,128)(2,1)S(1)}, bf16[8,16,640]{2,1,0:T(8,128)(2,1)S(1)}, u32[]{:S(2)}, u32[]{:S(2)}) %collective-permute-start.6) | collective-permute-done | bytes 163872 | tf_op jit(solution)/shard_map/ppermute | solution.py:276
  37.0 1.3 %temporal2.1 = (bf16[1,4,2,8,16,640]{5,4,3,2,1,0:T(8,128)(2,1)}, bf16[2,8,16,640]{3,2,1,0:T(8,128)(2,1)S(1)}) custom-call(bf16[2,8,16,640]{3,2,1,0:T(8,128)(2,1)S(1)} %get-tuple-element.54.refs_0_, bf16[2,8,16,640]{3,2,1,0:T(8,128)(2,1)S(1)} %get-tuple-element.55.refs_1_, ...), custom_call_target="tpu_custom_call", output_to_operand_aliasing={{0}: (6, {})} | custom-call | flops 629145600 | bytes 2457600 | tf_op jit(solution)/shard_map/temporal2/pallas_call | solution.py:214
  38.3 1.0 %collective-permute-start.8 = (bf16[2,8,16,640]{3,2,1,0:T(8,128)(2,1)S(1)}, bf16[2,8,16,640]{3,2,1,0:T(8,128)(2,1)S(1)}, u32[]{:S(2)}, u32[]{:S(2)}) collective-permute-start(bf16[2,8,16,640]{3,2,1,0:T(8,128)(2,1)S(1)} %get-tuple-element.58.refs_5_), channel_id=1, source_target_pairs={{0,8},{8,0},{1,9},{9,1},{2,10},{10,2},{3,11},{11,3},{4,12},{12,4},... | collective-permute-start | bytes 983048 | tf_op jit(solution)/shard_map/ppermute | solution.py:269
  39.3 0.0 collective-permute-start.11
  39.4 1.3 %collective-permute-start.12 = (bf16[8,16,640]{2,1,0:T(8,128)(2,1)S(1)}, bf16[8,16,640]{2,1,0:T(8,128)(2,1)S(1)}, u32[]{:S(2)}, u32[]{:S(2)}) collective-permute-start(bf16[8,16,640]{2,1,0:T(8,128)(2,1)S(1)} %get-tuple-element.66), channel_id=1, source_target_pairs={{0,8},{1,2},{2,1},{3,4},{4,3},{5,6},{6,5},{7,15},{8,0},{9,10},{10,... | collective-permute-start | bytes 491528 | tf_op jit(solution)/shard_map/ppermute | solution.py:277
  40.7 0.0 collective-permute-done.8.refs_1_
  40.7 2.9 %spatial4.1 = (bf16[2,8,16,640]{3,2,1,0:T(8,128)(2,1)S(1)}, bf16[2,8,16,640]{3,2,1,0:T(8,128)(2,1)S(1)}, bf16[8,16,640]{2,1,0:T(8,128)(2,1)S(1)}, bf16[8,16,640]{2,1,0:T(8,128)(2,1)S(1)}) custom-call(bf16[3,2,8,16,640]{4,3,2,1,0:T(8,128)(2,1)S(1)} %copy-done, bf16[2,8,16,640]{3,2,1,0:T(8,128)(2,1)S(1)} %collective-permute-done.8.refs_1_, ...), custom_call_target="tpu_custom_call" | custom-call | flops 1887436800 | bytes 7372800 | tf_op jit(solution)/shard_map/spatial4/pallas_call | solution.py:183
  43.6 1.1 %collective-permute-start.10 = (bf16[8,16,640]{2,1,0:T(8,128)(2,1)S(1)}, bf16[8,16,640]{2,1,0:T(8,128)(2,1)S(1)}, u32[]{:S(2)}, u32[]{:S(2)}) collective-permute-start(bf16[8,16,640]{2,1,0:T(8,128)(2,1)S(1)} %get-tuple-element.62), channel_id=1, source_target_pairs={{0,8},{1,17},{2,18},{3,19},{4,20},{5,21},{6,22},{7,15},{8,0},{9,10... | collective-permute-start | bytes 491528 | tf_op jit(solution)/shard_map/ppermute | solution.py:277
  44.7 0.0 collective-permute-start.9
  44.7 1.2 %collective-permute-done.12.refs_3_ = bf16[8,16,640]{2,1,0:T(8,128)(2,1)S(1)} collective-permute-done((bf16[8,16,640]{2,1,0:T(8,128)(2,1)S(1)}, bf16[8,16,640]{2,1,0:T(8,128)(2,1)S(1)}, u32[]{:S(2)}, u32[]{:S(2)}) %collective-permute-start.12) | collective-permute-done | bytes 163872 | tf_op jit(solution)/shard_map/ppermute | solution.py:277
  45.9 4.4 %collective-permute-done.11.refs_2_ = bf16[8,16,640]{2,1,0:T(8,128)(2,1)S(1)} collective-permute-done((bf16[8,16,640]{2,1,0:T(8,128)(2,1)S(1)}, bf16[8,16,640]{2,1,0:T(8,128)(2,1)S(1)}, u32[]{:S(2)}, u32[]{:S(2)}) %collective-permute-start.11) | collective-permute-done | bytes 163872 | tf_op jit(solution)/shard_map/ppermute | solution.py:276
  50.3 1.3 %temporal3.1 = (bf16[1,4,2,8,16,640]{5,4,3,2,1,0:T(8,128)(2,1)}, bf16[2,8,16,640]{3,2,1,0:T(8,128)(2,1)S(1)}) custom-call(bf16[2,8,16,640]{3,2,1,0:T(8,128)(2,1)S(1)} %get-tuple-element.64.refs_0_, bf16[2,8,16,640]{3,2,1,0:T(8,128)(2,1)S(1)} %get-tuple-element.65.refs_1_, ...), custom_call_target="tpu_custom_call", output_to_operand_aliasing={{0}: (6, {})} | custom-call | flops 629145600 | bytes 2457600 | tf_op jit(solution)/shard_map/temporal3/pallas_call | solution.py:214
  51.6 0.0 collective-permute-done.10.refs_3_
  51.6 0.7 %collective-permute-done.9.refs_2_ = bf16[8,16,640]{2,1,0:T(8,128)(2,1)S(1)} collective-permute-done((bf16[8,16,640]{2,1,0:T(8,128)(2,1)S(1)}, bf16[8,16,640]{2,1,0:T(8,128)(2,1)S(1)}, u32[]{:S(2)}, u32[]{:S(2)}) %collective-permute-start.9) | collective-permute-done | bytes 163872 | tf_op jit(solution)/shard_map/ppermute | solution.py:276
  52.3 2.5 %temporal4.1 = (bf16[1,4,2,8,16,640]{5,4,3,2,1,0:T(8,128)(2,1)}, bf16[2,8,16,640]{3,2,1,0:T(8,128)(2,1)}) custom-call(bf16[2,8,16,640]{3,2,1,0:T(8,128)(2,1)S(1)} %get-tuple-element.59.refs_0_, bf16[2,8,16,640]{3,2,1,0:T(8,128)(2,1)S(1)} %get-tuple-element.60.refs_1_, ...), custom_call_target="tpu_custom_call", output_to_operand_aliasing={{0}: (6, {})} | custom-call | flops 629145600 | bytes 2457600 | tf_op jit(solution)/shard_map/temporal4/pallas_call | solution.py:214
  (1 shorter events, 0.0 us)
Async XLA Ops:
  0.0 1.0 %copy-start.2 = (bf16[1,2,8,16,640]{4,3,2,1,0:T(8,128)(2,1)S(1)}, bf16[1,2,8,16,640]{4,3,2,1,0:T(8,128)(2,1)}, u32[]{:S(2)}) copy-start(bf16[1,2,8,16,640]{4,3,2,1,0:T(8,128)(2,1)} %param.6) | copy-start | bytes 983044
  1.0 0.7 %copy-start.3 = (f32[1,5,640]{2,0,1:T(1,128)S(1)}, f32[1,5,640]{2,0,1:T(1,128)}, u32[]{:S(2)}) copy-start(f32[1,5,640]{2,0,1:T(1,128)} %param.9) | copy-start | bytes 38404
  1.7 6.8 %copy-start = (bf16[3,2,8,16,640]{4,3,2,1,0:T(8,128)(2,1)S(1)}, bf16[3,2,8,16,640]{4,3,2,1,0:T(8,128)(2,1)}, u32[]{:S(2)}) copy-start(bf16[3,2,8,16,640]{4,3,2,1,0:T(8,128)(2,1)} %refs_0_.7) | copy-start | bytes 2949124
  1.7 6.8 %copy-start.4 = (f32[1,5,640]{2,0,1:T(1,128)S(1)}, f32[1,5,640]{2,0,1:T(1,128)}, u32[]{:S(2)}) copy-start(f32[1,5,640]{2,0,1:T(1,128)} %param.9) | copy-start | bytes 38404
  7.0 4.9 %collective-permute-start = (bf16[8,16,640]{2,1,0:T(8,128)(2,1)S(1)}, bf16[8,16,640]{2,1,0:T(8,128)(2,1)S(1)}, u32[]{:S(2)}, u32[]{:S(2)}) collective-permute-start(bf16[8,16,640]{2,1,0:T(8,128)(2,1)S(1)} %get-tuple-element.43), channel_id=1, source_target_pairs={{0,1},{1,0},{2,3},{3,2},{4,5},{5,4},{6,7},{7,6},{8,24},{9,25},{10,... | collective-permute-start | bytes 491528 | tf_op jit(solution)/shard_map/ppermute | solution.py:276
  7.3 5.7 %collective-permute-start.1 = (bf16[8,16,640]{2,1,0:T(8,128)(2,1)S(1)}, bf16[8,16,640]{2,1,0:T(8,128)(2,1)S(1)}, u32[]{:S(2)}, u32[]{:S(2)}) collective-permute-start(bf16[8,16,640]{2,1,0:T(8,128)(2,1)S(1)} %get-tuple-element.44), channel_id=1, source_target_pairs={{0,8},{1,2},{2,1},{3,4},{4,3},{5,6},{6,5},{7,15},{8,0},{9,25},{10,... | collective-permute-start | bytes 491528 | tf_op jit(solution)/shard_map/ppermute | solution.py:277
  8.5 3.0 %copy-start.1 = (bf16[1,3,640,640]{3,2,1,0:T(8,128)(2,1)S(1)}, bf16[1,3,640,640]{3,2,1,0:T(8,128)(2,1)}, u32[]{:S(2)}) copy-start(bf16[1,3,640,640]{3,2,1,0:T(8,128)(2,1)} %param.10) | copy-start | bytes 7372804
  8.5 3.0 %copy-start.5 = (f32[1,5,640]{2,0,1:T(1,128)S(1)}, f32[1,5,640]{2,0,1:T(1,128)}, u32[]{:S(2)}) copy-start(f32[1,5,640]{2,0,1:T(1,128)} %param.11) | copy-start | bytes 38404
  14.1 3.9 %collective-permute-start.2 = (bf16[2,8,16,640]{3,2,1,0:T(8,128)(2,1)S(1)}, bf16[2,8,16,640]{3,2,1,0:T(8,128)(2,1)S(1)}, u32[]{:S(2)}, u32[]{:S(2)}) collective-permute-start(bf16[2,8,16,640]{3,2,1,0:T(8,128)(2,1)S(1)} %get-tuple-element.45.refs_5_), channel_id=1, source_target_pairs={{0,8},{8,0},{1,9},{9,1},{2,10},{10,2},{3,11},{11,3},{4,12},{12,4},... | collective-permute-start | bytes 983048 | tf_op jit(solution)/shard_map/ppermute | solution.py:269
  16.6 9.2 %collective-permute-start.3 = (bf16[8,16,640]{2,1,0:T(8,128)(2,1)S(1)}, bf16[8,16,640]{2,1,0:T(8,128)(2,1)S(1)}, u32[]{:S(2)}, u32[]{:S(2)}) collective-permute-start(bf16[8,16,640]{2,1,0:T(8,128)(2,1)S(1)} %get-tuple-element.40), channel_id=1, source_target_pairs={{0,1},{1,0},{2,3},{3,2},{4,5},{5,4},{6,7},{7,6},{8,9},{9,8},{10,11... | collective-permute-start | bytes 491528 | tf_op jit(solution)/shard_map/ppermute | solution.py:276
  16.6 6.5 %collective-permute-start.4 = (bf16[8,16,640]{2,1,0:T(8,128)(2,1)S(1)}, bf16[8,16,640]{2,1,0:T(8,128)(2,1)S(1)}, u32[]{:S(2)}, u32[]{:S(2)}) collective-permute-start(bf16[8,16,640]{2,1,0:T(8,128)(2,1)S(1)} %get-tuple-element.51), channel_id=1, source_target_pairs={{0,8},{1,2},{2,1},{3,4},{4,3},{5,6},{6,5},{7,15},{8,0},{9,10},{10,... | collective-permute-start | bytes 491528 | tf_op jit(solution)/shard_map/ppermute | solution.py:277
  26.9 2.4 %collective-permute-start.5 = (bf16[2,8,16,640]{3,2,1,0:T(8,128)(2,1)S(1)}, bf16[2,8,16,640]{3,2,1,0:T(8,128)(2,1)S(1)}, u32[]{:S(2)}, u32[]{:S(2)}) collective-permute-start(bf16[2,8,16,640]{3,2,1,0:T(8,128)(2,1)S(1)} %get-tuple-element.52.refs_5_), channel_id=1, source_target_pairs={{0,8},{8,0},{1,9},{9,1},{2,10},{10,2},{3,11},{11,3},{4,12},{12,4},... | collective-permute-start | bytes 983048 | tf_op jit(solution)/shard_map/ppermute | solution.py:269
  27.9 9.2 %collective-permute-start.6 = (bf16[8,16,640]{2,1,0:T(8,128)(2,1)S(1)}, bf16[8,16,640]{2,1,0:T(8,128)(2,1)S(1)}, u32[]{:S(2)}, u32[]{:S(2)}) collective-permute-start(bf16[8,16,640]{2,1,0:T(8,128)(2,1)S(1)} %get-tuple-element.48), channel_id=1, source_target_pairs={{0,1},{1,0},{2,3},{3,2},{4,5},{5,4},{6,7},{7,6},{8,9},{9,8},{10,11... | collective-permute-start | bytes 491528 | tf_op jit(solution)/shard_map/ppermute | solution.py:276
  27.9 6.5 %collective-permute-start.7 = (bf16[8,16,640]{2,1,0:T(8,128)(2,1)S(1)}, bf16[8,16,640]{2,1,0:T(8,128)(2,1)S(1)}, u32[]{:S(2)}, u32[]{:S(2)}) collective-permute-start(bf16[8,16,640]{2,1,0:T(8,128)(2,1)S(1)} %get-tuple-element.56), channel_id=1, source_target_pairs={{0,8},{1,2},{2,1},{3,4},{4,3},{5,6},{6,5},{7,15},{8,0},{9,10},{10,... | collective-permute-start | bytes 491528 | tf_op jit(solution)/shard_map/ppermute | solution.py:277
  38.3 2.4 %collective-permute-start.8 = (bf16[2,8,16,640]{3,2,1,0:T(8,128)(2,1)S(1)}, bf16[2,8,16,640]{3,2,1,0:T(8,128)(2,1)S(1)}, u32[]{:S(2)}, u32[]{:S(2)}) collective-permute-start(bf16[2,8,16,640]{3,2,1,0:T(8,128)(2,1)S(1)} %get-tuple-element.58.refs_5_), channel_id=1, source_target_pairs={{0,8},{8,0},{1,9},{9,1},{2,10},{10,2},{3,11},{11,3},{4,12},{12,4},... | collective-permute-start | bytes 983048 | tf_op jit(solution)/shard_map/ppermute | solution.py:269
  39.3 10.9 %collective-permute-start.11 = (bf16[8,16,640]{2,1,0:T(8,128)(2,1)S(1)}, bf16[8,16,640]{2,1,0:T(8,128)(2,1)S(1)}, u32[]{:S(2)}, u32[]{:S(2)}) collective-permute-start(bf16[8,16,640]{2,1,0:T(8,128)(2,1)S(1)} %get-tuple-element.53), channel_id=1, source_target_pairs={{0,1},{1,0},{2,3},{3,2},{4,5},{5,4},{6,7},{7,6},{8,9},{9,8},{10,11... | collective-permute-start | bytes 491528 | tf_op jit(solution)/shard_map/ppermute | solution.py:276
  39.4 6.5 %collective-permute-start.12 = (bf16[8,16,640]{2,1,0:T(8,128)(2,1)S(1)}, bf16[8,16,640]{2,1,0:T(8,128)(2,1)S(1)}, u32[]{:S(2)}, u32[]{:S(2)}) collective-permute-start(bf16[8,16,640]{2,1,0:T(8,128)(2,1)S(1)} %get-tuple-element.66), channel_id=1, source_target_pairs={{0,8},{1,2},{2,1},{3,4},{4,3},{5,6},{6,5},{7,15},{8,0},{9,10},{10,... | collective-permute-start | bytes 491528 | tf_op jit(solution)/shard_map/ppermute | solution.py:277
  43.6 8.0 %collective-permute-start.10 = (bf16[8,16,640]{2,1,0:T(8,128)(2,1)S(1)}, bf16[8,16,640]{2,1,0:T(8,128)(2,1)S(1)}, u32[]{:S(2)}, u32[]{:S(2)}) collective-permute-start(bf16[8,16,640]{2,1,0:T(8,128)(2,1)S(1)} %get-tuple-element.62), channel_id=1, source_target_pairs={{0,8},{1,17},{2,18},{3,19},{4,20},{5,21},{6,22},{7,15},{8,0},{9,10... | collective-permute-start | bytes 491528 | tf_op jit(solution)/shard_map/ppermute | solution.py:277
  44.7 7.6 %collective-permute-start.9 = (bf16[8,16,640]{2,1,0:T(8,128)(2,1)S(1)}, bf16[8,16,640]{2,1,0:T(8,128)(2,1)S(1)}, u32[]{:S(2)}, u32[]{:S(2)}) collective-permute-start(bf16[8,16,640]{2,1,0:T(8,128)(2,1)S(1)} %get-tuple-element.61), channel_id=1, source_target_pairs={{0,16},{1,17},{2,18},{3,19},{4,20},{5,21},{6,22},{7,23},{8,9},{9,8... | collective-permute-start | bytes 491528 | tf_op jit(solution)/shard_map/ppermute | solution.py:276
